TPU v7x, 32 devices: a whole 2x2x4 slice. The times are simulated.
32 devices in a mesh: pair: 8 (over z, x), row: 4 (over y, core).
Axes of the slice: x: 2, y: 2, z: 4, core: 2. Of those that a mesh axis runs over, the one named last changes fastest.
Arguments:
- records: bfloat16 [128, 4096, 8], P('row', 'pair'), may hold values from -10 to 10
- offsets: float32 [8, 128], P('pair', 'row'), may hold values from -1 to 1
- counts: int32 [8], replicated, may hold values from 64 to 128, as said below
- damping: float32 [1], replicated, may hold values from 0.1 to 1
Outputs:
- offset_step: float32 [8, 128], P('pair', 'row')
Inputs may be any that keep to these rules, and one draw needn't show every extreme that they name: Channel i of block b is live when i < counts[b]; in every draw some block has all 128 channels live.
All inputs are finite; a program needn't handle non-finite values.
Results may differ from a plain program's by a relative error of at most 0.0044.
Values may be sent and summed in bfloat16 or wider, within the bound.
No kernel may reach another device: no remote copies, remote signals or barrier semaphores. Data moves between devices by JAX's collectives and lax.ppermute only.
A program may use at most 64 MiB of HBM per device.

v0:
```python
import math

import jax
import jax.numpy as jnp
from jax import lax
from jax.sharding import PartitionSpec as P

CB = 128
NF = 512
NLAG = 256


def band_table(row_start, row_count, samples, first_bin, freq_count):
    sample_ids = row_start + jnp.arange(row_count, dtype=jnp.int32)
    freq_bins = first_bin + jnp.arange(freq_count, dtype=jnp.int32)
    phase_ids = sample_ids[:, None] * freq_bins[None, :] % samples
    angles = phase_ids.astype(jnp.float32) * (2.0 * math.pi / samples)
    return jnp.concatenate([jnp.cos(angles), jnp.sin(angles)], axis=1)


def lag_weights(samples, first_bin, freq_count, lag_count):
    freq_bins = first_bin + jnp.arange(freq_count, dtype=jnp.int32)
    lag_ids = 1 + jnp.arange(lag_count, dtype=jnp.int32)
    phase_ids = freq_bins[:, None] * lag_ids[None, :] % samples
    angles = phase_ids.astype(jnp.float32) * (2.0 * math.pi / samples)
    centre = (jnp.arange(freq_count, dtype=jnp.float32) + 0.5) * (math.pi / freq_count)
    weight = jnp.sin(centre) ** 2
    return (-2.0 * weight[:, None] * jnp.sin(angles)).astype(jnp.bfloat16)


def pair_stats(own_spec, partners, lag_table, angular):
    own_re = own_spec[:, 0].astype(jnp.float32)
    own_im = own_spec[:, 1].astype(jnp.float32)
    far_re = partners[:, :, 0].astype(jnp.float32)
    far_im = partners[:, :, 1].astype(jnp.float32)
    cross_re = own_re * far_re + own_im * far_im
    cross_im = own_im * far_re - own_re * far_im
    stacked = jnp.stack([cross_im, angular * cross_re]).astype(jnp.bfloat16)
    lagged = jnp.dot(stacked, lag_table, preferred_element_type=jnp.float32)
    residual = lagged[0]
    jacobian = lagged[1]
    return (jnp.sum(jacobian * jacobian, axis=-1), jnp.sum(jacobian * residual, axis=-1))


def per_device(records, offsets, counts, damping):
    nblock = lax.axis_size("pair")
    block_rank = lax.axis_index("pair")
    quarter = lax.axis_index("row")
    relaid = lax.all_to_all(records, "pair", split_axis=2, concat_axis=1, tiled=True)
    signal = relaid[:, :, 0]
    channels = signal.shape[0]
    samples = signal.shape[1]
    first_bin = samples // 8
    block_len = samples // 8

    def accumulate(partial_value, turn_index):
        first_row = turn_index * block_len
        segment = lax.dynamic_slice_in_dim(signal, first_row, block_len, 1)
        dft_table = band_table(first_row, block_len, samples, first_bin, NF)
        table_high = dft_table.astype(jnp.bfloat16)
        table_low = (dft_table - table_high.astype(jnp.float32)).astype(jnp.bfloat16)
        partial_value = partial_value + jnp.dot(
            segment, table_high, preferred_element_type=jnp.float32
        )
        partial_value = partial_value + jnp.dot(
            segment, table_low, preferred_element_type=jnp.float32
        )
        return (partial_value, None)

    spectrum, _ = lax.scan(
        accumulate, jnp.zeros((channels, 2 * NF), jnp.float32), jnp.arange(8, dtype=jnp.int32)
    )
    cosine_part = spectrum[:, :NF]
    sine_part = spectrum[:, NF:]
    angular = (first_bin + jnp.arange(NF, dtype=jnp.int32)).astype(jnp.float32) * (
        2.0 * math.pi / samples
    )
    shift_angle = offsets[0][:, None] * angular[None, :]
    shift_cos = jnp.cos(shift_angle)
    shift_sin = jnp.sin(shift_angle)
    real_part = cosine_part * shift_cos + sine_part * shift_sin
    imag_part = cosine_part * shift_sin - sine_part * shift_cos
    live_count = lax.dynamic_index_in_dim(counts, block_rank, keepdims=False)
    channel_ids = quarter * channels + jnp.arange(channels, dtype=jnp.int32)
    alive = (channel_ids < live_count).astype(jnp.float32)
    energy = jnp.mean(real_part * real_part + imag_part * imag_part, axis=1)
    weight_scale = alive / jnp.sqrt(energy + 1e-06)
    own_spec = jnp.stack(
        [real_part * weight_scale[:, None], imag_part * weight_scale[:, None]], axis=1
    ).astype(jnp.bfloat16)
    lag_table = lag_weights(samples, first_bin, NF, NLAG)
    segment = lax.all_gather(own_spec[None], "pair", axis=0, tiled=True)
    squares_part, products_part = pair_stats(own_spec, segment, lag_table, angular)
    partner_ids = jnp.arange(segment.shape[0], dtype=jnp.int32)
    keep_mask = (partner_ids > block_rank).astype(jnp.float32)[:, None]
    new_squares = squares_part * keep_mask
    new_products = products_part * keep_mask
    eye_blocks = jnp.eye(nblock, dtype=jnp.float32)
    onehot = (jnp.arange(nblock, dtype=jnp.int32) == block_rank).astype(jnp.float32)
    sq_t = new_squares.T
    pr_t = new_products.T
    crossing = sq_t[:, None, :] * onehot[None, :, None]
    diag_vals = sq_t + onehot[None, :] * jnp.sum(sq_t, axis=1, keepdims=True)
    hessian = diag_vals[:, :, None] * eye_blocks[None] - crossing - jnp.swapaxes(crossing, 1, 2)
    gradient = onehot[None, :] * jnp.sum(pr_t, axis=1, keepdims=True) - pr_t
    hessian, gradient = lax.psum((hessian, gradient), "pair")
    diagonal = jnp.diagonal(hessian, axis1=1, axis2=2)
    trace_sum = lax.psum(jnp.sum(diagonal), "row")
    level_mean = trace_sum / (nblock * CB)
    damped = damping[0] * (diagonal + level_mean)
    system = hessian + damped[:, :, None] * eye_blocks[None]
    factor = jnp.linalg.cholesky(system)
    update = -jax.scipy.linalg.cho_solve((factor, True), gradient[:, :, None])[:, :, 0]
    return lax.dynamic_slice_in_dim(update, block_rank, 1, 1).T


def solution(mesh):
    return jax.shard_map(
        per_device,
        mesh=mesh,
        in_specs=(P("row", "pair", None), P("pair", "row"), P(), P()),
        out_specs=P("pair", "row"),
        check_vma=False,
    )
```

profile of v0, /device:TPU:0, one launch (start us, length us, event | category | flops | bytes accessed | tf_op | source)
XLA Modules:
  0.0 172.0 jit_solution(3710374380044799579)
XLA Ops:
  0.0 1.7 %copy.35 = bf16[32,512,8]{1,0,2:T(8,128)(2,1)} copy(bf16[32,512,8]{1,2,0:T(8,128)(2,1)} %param.6) | data formatting | bytes 524288 | tf_op args[0]
  1.7 7.3 %all-to-all-start = ((bf16[32,512,8]{1,0,2:T(8,128)(2,1)}), bf16[32,512,8]{1,0,2:T(8,128)(2,1)S(1)}, u32[]{:S(2)}, u32[]{:S(2)}) async-start(bf16[32,512,8]{1,0,2:T(8,128)(2,1)} %copy.35), calls=%async_computation | async-start | bytes 524288 | tf_op jit(solution)/shard_map/all_to_all | solution.py:49
  9.2 0.6 dynamic_slice.20
  9.9 8.1 %all-to-all-done = bf16[32,512,8]{1,0,2:T(8,128)(2,1)S(1)} async-done(((bf16[32,512,8]{1,0,2:T(8,128)(2,1)}), bf16[32,512,8]{1,0,2:T(8,128)(2,1)S(1)}, u32[]{:S(2)}, u32[]{:S(2)}) %all-to-all-start) | async-done | bytes 262176 | tf_op jit(solution)/shard_map/all_to_all | solution.py:49
  18.0 48.9 %while.13 = (s32[]{:T(128)}, f32[32,1024]{1,0:T(8,128)S(1)}, s32[8]{0:T(128)S(1)}, bf16[32,4096]{1,0:T(8,128)(2,1)S(1)}, s32[]{:T(128)}, /*index=5*/s32[1]{0:T(128)}, s32[]{:T(128)}, s32[]{:T(128)}) while((s32[]{:T(128)}, f32[32,1024]{1,0:T(8,128)S(1)}, s32[8]{0:T(128)S(1)}, bf16[32,4096]{1,0:T(8,128)(2,1)S(1)}, s32[]{:T(128)}, ...), condition=%wide.region_1.2_spmd.clone, body=%wide.region_0.1_spmd.clone.sunk | while | flops 75596808 | bytes 6889645 | solution.py:70
  18.0 0.7 dynamic_slice.34
  19.4 4.1 %fusion.70 = (f32[512,512]{1,0:T(8,128)S(1)}, f32[512,512]{1,0:T(8,128)S(1)}) fusion(s32[512]{0:T(512)S(1)} %get-tuple-element.138, s32[512]{0:T(512)S(1)} %get-tuple-element.139), kind=kLoop, calls=%fused_computation.16.clone.1 | loop fusion | flops 3670016 | bytes 2101248 | tf_op jit(solution)/shard_map/while/body/eval_jaxpr/cos | solution.py:18
  23.5 0.3 fusion.71
  23.8 0.3 convolution_add_fusion.2
  24.1 0.7 dynamic_slice.34
  25.5 4.1 %fusion.70 = (f32[512,512]{1,0:T(8,128)S(1)}, f32[512,512]{1,0:T(8,128)S(1)}) fusion(s32[512]{0:T(512)S(1)} %get-tuple-element.138, s32[512]{0:T(512)S(1)} %get-tuple-element.139), kind=kLoop, calls=%fused_computation.16.clone.1 | loop fusion | flops 3670016 | bytes 2101248 | tf_op jit(solution)/shard_map/while/body/eval_jaxpr/cos | solution.py:18
  29.6 0.3 fusion.71
  29.9 0.3 convolution_add_fusion.2
  30.2 0.7 dynamic_slice.34
  31.6 4.1 %fusion.70 = (f32[512,512]{1,0:T(8,128)S(1)}, f32[512,512]{1,0:T(8,128)S(1)}) fusion(s32[512]{0:T(512)S(1)} %get-tuple-element.138, s32[512]{0:T(512)S(1)} %get-tuple-element.139), kind=kLoop, calls=%fused_computation.16.clone.1 | loop fusion | flops 3670016 | bytes 2101248 | tf_op jit(solution)/shard_map/while/body/eval_jaxpr/cos | solution.py:18
  35.8 0.3 fusion.71
  36.1 0.3 convolution_add_fusion.2
  36.3 0.7 dynamic_slice.34
  37.7 4.1 %fusion.70 = (f32[512,512]{1,0:T(8,128)S(1)}, f32[512,512]{1,0:T(8,128)S(1)}) fusion(s32[512]{0:T(512)S(1)} %get-tuple-element.138, s32[512]{0:T(512)S(1)} %get-tuple-element.139), kind=kLoop, calls=%fused_computation.16.clone.1 | loop fusion | flops 3670016 | bytes 2101248 | tf_op jit(solution)/shard_map/while/body/eval_jaxpr/cos | solution.py:18
  41.9 0.3 fusion.71
  42.2 0.3 convolution_add_fusion.2
  42.5 0.7 dynamic_slice.34
  43.8 4.1 %fusion.70 = (f32[512,512]{1,0:T(8,128)S(1)}, f32[512,512]{1,0:T(8,128)S(1)}) fusion(s32[512]{0:T(512)S(1)} %get-tuple-element.138, s32[512]{0:T(512)S(1)} %get-tuple-element.139), kind=kLoop, calls=%fused_computation.16.clone.1 | loop fusion | flops 3670016 | bytes 2101248 | tf_op jit(solution)/shard_map/while/body/eval_jaxpr/cos | solution.py:18
  48.0 0.3 fusion.71
  48.3 0.3 convolution_add_fusion.2
  48.6 0.7 dynamic_slice.34
  50.0 4.1 %fusion.70 = (f32[512,512]{1,0:T(8,128)S(1)}, f32[512,512]{1,0:T(8,128)S(1)}) fusion(s32[512]{0:T(512)S(1)} %get-tuple-element.138, s32[512]{0:T(512)S(1)} %get-tuple-element.139), kind=kLoop, calls=%fused_computation.16.clone.1 | loop fusion | flops 3670016 | bytes 2101248 | tf_op jit(solution)/shard_map/while/body/eval_jaxpr/cos | solution.py:18
  54.1 0.3 fusion.71
  54.4 0.3 convolution_add_fusion.2
  54.7 0.7 dynamic_slice.34
  56.1 4.1 %fusion.70 = (f32[512,512]{1,0:T(8,128)S(1)}, f32[512,512]{1,0:T(8,128)S(1)}) fusion(s32[512]{0:T(512)S(1)} %get-tuple-element.138, s32[512]{0:T(512)S(1)} %get-tuple-element.139), kind=kLoop, calls=%fused_computation.16.clone.1 | loop fusion | flops 3670016 | bytes 2101248 | tf_op jit(solution)/shard_map/while/body/eval_jaxpr/cos | solution.py:18
  60.2 0.3 fusion.71
  60.5 0.3 convolution_add_fusion.2
  60.8 0.7 dynamic_slice.34
  62.2 4.1 %fusion.70 = (f32[512,512]{1,0:T(8,128)S(1)}, f32[512,512]{1,0:T(8,128)S(1)}) fusion(s32[512]{0:T(512)S(1)} %get-tuple-element.138, s32[512]{0:T(512)S(1)} %get-tuple-element.139), kind=kLoop, calls=%fused_computation.16.clone.1 | loop fusion | flops 3670016 | bytes 2101248 | tf_op jit(solution)/shard_map/while/body/eval_jaxpr/cos | solution.py:18
  66.4 0.3 fusion.71
  66.6 0.3 convolution_add_fusion.2
  66.9 0.4 add_reduce_fusion
  67.4 0.6 compare_select_fusion
  68.1 31.6 %all_gather.3 = bf16[8,32,2,512]{3,1,0,2:T(8,128)(2,1)S(1)} all-gather(bf16[1,32,2,512]{3,1,0,2:T(8,128)(2,1)S(1)} %pad_maximum_fusion.1), channel_id=1, replica_groups=mesh['pair'=8,'row'=4] {'pair'}, dimensions={0}, use_global_device_ids=true | all-gather | bytes 589824 | tf_op jit(solution)/shard_map/all_gather | solution.py:92
  99.9 2.3 %fusion.28 = f32[2,8,32,256]{3,2,1,0:T(8,128)S(1)} fusion(bf16[1,8,32,512]{3,2,1,0:T(8,128)(2,1)S(1)} %get-tuple-element.99, bf16[1,8,32,512]{3,2,1,0:T(8,128)(2,1)S(1)} %get-tuple-element.98, s32[256]{0:T(256)S(1)} %iota_add_fusion.3, s32[512]{0:T(512)S(1)} %iota_add_fusion.2, f32[512]{0:T(512)S(1)} %multiply_multiply_fusion), kind=kOutput, calls=%fused_computation.45 | convolution fusion | flops 136577024 | bytes 1053696 | tf_op jit(solution)/shard_map/dot_general | solution.py:39
  102.6 35.2 %all-reduce = (f32[32,8,8]{0,1,2:T(8,128)S(1)}, f32[32,8]{0,1:T(8,128)S(1)}) all-reduce(f32[32,8,8]{0,1,2:T(8,128)S(1)} %multiply_subtract_fusion, f32[32,8]{0,1:T(8,128)S(1)} %get-tuple-element.104), channel_id=1, replica_groups=mesh['pair'=8,'row'=4] {'pair'}, use_global_device_ids=true, to_apply=%region_5.6 | all-reduce | flops 2304 | bytes 18432 | tf_op jit(solution)/shard_map/psum | solution.py:106
  137.8 0.6 gather_fusion
  138.4 0.7 reduce_sum.57
  139.7 6.3 %psum.22 = f32[]{:T(128)} all-reduce(f32[]{:T(128)} %reduce_sum.57), channel_id=1, replica_groups=mesh['pair'=8,'row'=4] {'row'}, use_global_device_ids=true, to_apply=%region_7.8 | all-reduce | flops 1 | bytes 8 | tf_op jit(solution)/shard_map/psum | solution.py:108
  146.9 23.5 %custom-call.11 = f32[32,8,8]{2,1,0:T(8,128)S(1)} custom-call(f32[32,8,8]{2,1,0:T(8,128)S(1)} %broadcast_multiply_fusion), custom_call_target="Cholesky" | custom-call | tf_op jit(solution)/shard_map/jit(cholesky)/cholesky | solution.py:112
  170.7 0.7 custom-call.12
  171.5 0.5 dynamic-slice_bitcast_fusion
  (45 shorter events, 1.5 us)
Async XLA Ops:
  0.0 9.2 %copy-start.1 = (s32[8]{0:T(128)S(1)}, s32[8]{0:T(128)}, u32[]{:S(2)}) copy-start(s32[8]{0:T(128)} %param.8) | copy-start | bytes 100
  1.7 16.2 %all-to-all-start = ((bf16[32,512,8]{1,0,2:T(8,128)(2,1)}), bf16[32,512,8]{1,0,2:T(8,128)(2,1)S(1)}, u32[]{:S(2)}, u32[]{:S(2)}) async-start(bf16[32,512,8]{1,0,2:T(8,128)(2,1)} %copy.35), calls=%async_computation | async-start | bytes 524288 | tf_op jit(solution)/shard_map/all_to_all | solution.py:49
  18.0 49.0 %copy-start = (f32[1,32]{1,0:T(1,128)S(1)}, f32[1,32]{1,0:T(1,128)}, u32[]{:S(2)}) copy-start(f32[1,32]{1,0:T(1,128)} %param.7) | copy-start | bytes 388
where the time goes:
time: 172 us
  blocking collectives  73.1 us (42%)
  other arithmetic  60.2 us (35%)
  local copies, waits for them, and re-layouts  9.21 us (5%)
  waiting for transfers between devices  8.06 us (5%)
  starting transfers between devices  7.28 us (4%)
  matrix products  6.83 us (4%)
  loops' own time  5.79 us (3%)
    psum x1, blocking collectives, per_device(): hessian, gradient = lax.psum((hessian, gradient), 'pair')  35.2 us
    cos x8, other arithmetic, band_table(): return jnp.concatenate([jnp.cos(angles), jnp.sin(angles)], axis=1)  33.2 us
    all_gather x1, blocking collectives, per_device(): segment = lax.all_gather(own_spec[None], 'pair', axis=0, tiled=True)  31.6 us
    another operation x4, other arithmetic, per_device(): factor = jnp.linalg.cholesky(system)  23.6 us
    all_to_all x1, waiting for transfers between devices, per_device(): lax.all_to_all(records, 'pair', split_axis=2, concat_axis=1, tiled=True)  8.06 us
    all_to_all x1, starting transfers between devices, per_device(): lax.all_to_all(records, 'pair', split_axis=2, concat_axis=1, tiled=True)  7.28 us
    psum x1, blocking collectives, per_device(): trace_sum = lax.psum(jnp.sum(diagonal), 'row')  6.25 us
    another operation x1, loops' own time, per_device(): lax.scan(accumulate, jnp.zeros((channels, 2 * NF), jnp.float32), jnp.aran...  5.79 us
  transfers between devices with their start and end apart: 1, of which 1 were waited for; matrix products, arithmetic and copies ran while one was open for 0% of the time, Pallas kernels for 0%

commit v1 on v0

--- a/solution.py
+++ b/solution.py
@@ -1,8 +1,11 @@
+import functools
 import math
 
 import jax
 import jax.numpy as jnp
 from jax import lax
+from jax.experimental import pallas as pl
+from jax.experimental.pallas import tpu as pltpu
 from jax.sharding import PartitionSpec as P
 
 CB = 128
@@ -42,7 +45,7 @@
     return (jnp.sum(jacobian * jacobian, axis=-1), jnp.sum(jacobian * residual, axis=-1))
 
 
-def per_device(records, offsets, counts, damping):
+def per_device_general(records, offsets, counts, damping):
     nblock = lax.axis_size("pair")
     block_rank = lax.axis_index("pair")
     quarter = lax.axis_index("row")
@@ -114,9 +117,288 @@
     return lax.dynamic_slice_in_dim(update, block_rank, 1, 1).T
 
 
+LANES = 128
+NBLOCK = 8
+REACH = NBLOCK // 2
+VMEM = pl.BlockSpec(memory_space=pltpu.VMEM)
+ANY = pl.BlockSpec(memory_space=pl.ANY)
+
+
+def pack_kernel(own, cols, rec_ref, off_ref, out_ref, wide, sems):
+    ndest = out_ref.shape[0]
+    copies = []
+    for dest in range(ndest):
+        for col in range(cols):
+            copies.append(
+                pltpu.make_async_copy(
+                    rec_ref.at[pl.ds(dest * own, own), :, pl.ds(col * LANES, LANES)],
+                    out_ref.at[dest, pl.ds(col * own, own)],
+                    sems.at[dest, col],
+                )
+            )
+            copies[-1].start()
+    channels = off_ref.shape[1]
+    wide[...] = jnp.zeros_like(wide)
+    wide[:, :channels] = jnp.broadcast_to(off_ref[...], (NBLOCK, channels))
+    value = wide[...]
+    high = value.astype(jnp.bfloat16).astype(jnp.float32)
+    middle = (value - high).astype(jnp.bfloat16).astype(jnp.float32)
+    low = value - high - middle
+    pieces = high + pltpu.roll(middle, channels, 1) + pltpu.roll(low, 2 * channels, 1)
+    for dest in range(ndest):
+        tile = pieces if dest == 0 else pltpu.roll(pieces, LANES - dest * own, 1)
+        out_ref[dest, cols * own] = tile.astype(jnp.bfloat16)
+    for copy in copies:
+        copy.wait()
+
+
+def sin_cos(angle):
+    square = angle * angle
+    sine = jnp.float32(-1.0 / 39916800.0)
+    for factor in (1.0 / 362880.0, -1.0 / 5040.0, 1.0 / 120.0, -1.0 / 6.0, 1.0):
+        sine = sine * square + jnp.float32(factor)
+    cosine = jnp.float32(1.0 / 479001600.0)
+    for factor in (-1.0 / 3628800.0, 1.0 / 40320.0, -1.0 / 720.0, 1.0 / 24.0, -0.5, 1.0):
+        cosine = cosine * square + jnp.float32(factor)
+    return sine * angle, cosine
+
+
+def stats_kernel(
+    own, cols, x_ref, high_ref, low_ref, turn_ref, ang_ref, lag_ref, live_ref, out_ref,
+    spectrum, re_ref, im_ref, stacked,
+):
+    shards = x_ref.shape[0]
+    rows = own * NBLOCK
+    signal = jnp.concatenate(
+        [
+            jnp.concatenate(
+                [
+                    jnp.concatenate(
+                        [x_ref[shard, col * own + c].astype(jnp.float32) for col in range(cols)],
+                        axis=1,
+                    )
+                    for c in range(own)
+                ],
+                axis=0,
+            )
+            for shard in range(shards)
+        ],
+        axis=0,
+    ).astype(jnp.bfloat16)
+    spectrum[...] = jnp.dot(
+        signal, high_ref[...], preferred_element_type=jnp.float32
+    ) + jnp.dot(signal, low_ref[...], preferred_element_type=jnp.float32)
+
+    block_ids = lax.broadcasted_iota(jnp.int32, (NBLOCK, LANES), 0)
+    pieces = jnp.zeros((NBLOCK, LANES), jnp.float32)
+    for shard in range(shards):
+        pieces = jnp.where(
+            block_ids == shard, x_ref[shard, cols * own].astype(jnp.float32), pieces
+        )
+    channels = own * shards
+    shift = (pieces + pltpu.roll(pieces, LANES - channels, 1)) + pltpu.roll(
+        pieces, LANES - 2 * channels, 1
+    )
+    energy = [jnp.zeros((NBLOCK, 1), jnp.float32)] * own
+    for col in range(NF // LANES):
+        at = pl.ds(col * LANES, LANES)
+        at_sine = pl.ds(NF + col * LANES, LANES)
+        cosine_part = spectrum[pl.ds(0, rows), at]
+        sine_part = spectrum[pl.ds(0, rows), at_sine]
+        for shard in range(1, shards):
+            turn_cos = turn_ref[pl.ds(shard, 1), at]
+            turn_sin = turn_ref[pl.ds(shard, 1), at_sine]
+            part_cos = spectrum[pl.ds(shard * rows, rows), at]
+            part_sin = spectrum[pl.ds(shard * rows, rows), at_sine]
+            cosine_part += turn_cos * part_cos - turn_sin * part_sin
+            sine_part += turn_sin * part_cos + turn_cos * part_sin
+        for c in range(own):
+            piece = slice(c * NBLOCK, (c + 1) * NBLOCK)
+            shift_sin, shift_cos = sin_cos(shift[:, c : c + 1] * ang_ref[:, at])
+            real = cosine_part[piece] * shift_cos + sine_part[piece] * shift_sin
+            imag = cosine_part[piece] * shift_sin - sine_part[piece] * shift_cos
+            energy[c] += jnp.sum(real * real + imag * imag, axis=1, keepdims=True)
+            re_ref[pl.ds(c * NBLOCK, NBLOCK), at] = real
+            im_ref[pl.ds(c * NBLOCK, NBLOCK), at] = imag
+
+    half = own * REACH * NBLOCK
+    angular = ang_ref[...]
+    for c in range(own):
+        at = pl.ds(c * NBLOCK, NBLOCK)
+        scale = live_ref[c][:, :1] / jnp.sqrt(energy[c] * (1.0 / NF) + 1e-06)
+        real = (re_ref[at, :] * scale).astype(jnp.bfloat16).astype(jnp.float32)
+        imag = (im_ref[at, :] * scale).astype(jnp.bfloat16).astype(jnp.float32)
+        crossings = []
+        for reach in range(1, REACH + 1):
+            far_re = pltpu.roll(real, NBLOCK - reach, 0)
+            far_im = pltpu.roll(imag, NBLOCK - reach, 0)
+            cross_re = real * far_re + imag * far_im
+            cross_im = imag * far_re - real * far_im
+            crossings.append((cross_im, angular * cross_re))
+        width = REACH * NBLOCK
+        for part in range(2):
+            stacked[pl.ds(part * half + c * width, width), :] = jnp.concatenate(
+                [crossing[part] for crossing in crossings], axis=0
+            ).astype(jnp.bfloat16)
+    lagged = lax.dot_general(
+        lag_ref[...], stacked[...], (((1,), (1,)), ((), ())), preferred_element_type=jnp.float32
+    )
+    residual = lagged[:, :half]
+    jacobian = lagged[:, half:]
+    squares = jnp.sum(jacobian * jacobian, axis=0, keepdims=True)
+    products = jnp.sum(jacobian * residual, axis=0, keepdims=True)
+    both = jnp.concatenate([squares, products], axis=0)
+    out_ref[...] = jnp.broadcast_to(both[None], out_ref.shape)
+
+
+def solve_kernel(own, total, got_ref, damp_ref, out_ref, steps):
+    shards = got_ref.shape[0]
+    quarter = lax.axis_index("row")
+    me = lax.axis_index("pair")
+    span = REACH * NBLOCK
+    lane_ids = lax.broadcasted_iota(jnp.int32, (NBLOCK, LANES), 1)
+    block_ids = lax.broadcasted_iota(jnp.int32, (NBLOCK, LANES), 0)
+
+    summed = jnp.zeros((1, LANES), jnp.float32)
+    for shard in range(shards):
+        for other in range(got_ref.shape[1]):
+            summed += got_ref[shard, other, 0:1, :]
+    inner = (lane_ids[:1] % span) < (REACH - 1) * NBLOCK
+    level = jnp.sum(jnp.where(inner, 2.0 * summed, summed), axis=1, keepdims=True) / total
+
+    squares = jnp.concatenate(
+        [got_ref[shard, quarter, 0:1, :] for shard in range(shards)], axis=0
+    )
+    products = jnp.concatenate(
+        [got_ref[shard, quarter, 1:2, :] for shard in range(shards)], axis=0
+    )
+
+    def entry(array, reach, block):
+        lane = (reach - 1) * NBLOCK + block
+        return array if lane == 0 else pltpu.roll(array, LANES - lane, 1)
+
+    weight = {}
+    slope = {}
+    for reach in range(1, REACH + 1):
+        for block in range(NBLOCK if reach < REACH else NBLOCK // 2):
+            far = (block + reach) % NBLOCK
+            value = entry(squares, reach, block)
+            weight[block, far] = value
+            weight[far, block] = value
+            value = entry(products, reach, block)
+            slope[block, far] = value
+            slope[far, block] = -value
+    damping = damp_ref[...]
+    matrix = {}
+    right = []
+    for a in range(NBLOCK):
+        others = [b for b in range(NBLOCK) if b != a]
+        diagonal = functools.reduce(lambda x, y: x + y, [weight[a, b] for b in others])
+        matrix[a, a] = diagonal + damping * (diagonal + level)
+        for b in range(a):
+            matrix[a, b] = -weight[a, b]
+        right.append(functools.reduce(lambda x, y: x + y, [slope[a, b] for b in others]))
+    inverse = []
+    for k in range(NBLOCK):
+        inverse.append(1.0 / matrix[k, k])
+        for i in range(k + 1, NBLOCK):
+            ratio = matrix[i, k] * inverse[k]
+            for j in range(k + 1, i + 1):
+                matrix[i, j] = matrix[i, j] - ratio * matrix[j, k]
+            right[i] = right[i] - ratio * right[k]
+    step = [None] * NBLOCK
+    for i in reversed(range(NBLOCK)):
+        value = right[i]
+        for j in range(i + 1, NBLOCK):
+            value = value - matrix[j, i] * step[j]
+        step[i] = value * inverse[i]
+        steps[i] = -step[i]
+    mine = steps[me]
+    placed = jnp.zeros((NBLOCK, LANES), jnp.float32)
+    for c in range(own):
+        column = jnp.broadcast_to(mine[:, c * span : c * span + 1], (NBLOCK, LANES))
+        placed = jnp.where(lane_ids == block_ids * own + c, column, placed)
+    out_ref[...] = jnp.sum(placed, axis=0, keepdims=True)[:, : out_ref.shape[1]]
+
+
+def per_device(records, offsets, counts, damping):
+    shards = lax.axis_size("pair")
+    rows = lax.axis_size("row")
+    me = lax.axis_index("pair")
+    quarter = lax.axis_index("row")
+    channels, length, _ = records.shape
+    samples = length * shards
+    first_bin = samples // 8
+    own = channels // shards
+    cols = length // LANES
+    tiles = own * cols + 1
+
+    payload = pl.pallas_call(
+        functools.partial(pack_kernel, own, cols),
+        out_shape=jax.ShapeDtypeStruct((shards, tiles, NBLOCK, LANES), jnp.bfloat16),
+        in_specs=[ANY, VMEM],
+        out_specs=VMEM,
+        scratch_shapes=[
+            pltpu.VMEM((NBLOCK, LANES), jnp.float32),
+            pltpu.SemaphoreType.DMA((shards, cols)),
+        ],
+        name="pack",
+    )(jnp.transpose(records, (0, 2, 1)), offsets)
+    received = lax.all_to_all(payload, "pair", split_axis=0, concat_axis=0, tiled=True)
+
+    table = band_table(0, length, samples, first_bin, NF)
+    table_high = table.astype(jnp.bfloat16)
+    table_low = (table - lax.reduce_precision(table, 8, 7)).astype(jnp.bfloat16)
+    turn_ids = length * jnp.arange(shards, dtype=jnp.int32)[:, None]
+    bins = first_bin + jnp.arange(NF, dtype=jnp.int32)
+    turn_angle = (turn_ids * bins[None, :] % samples).astype(jnp.float32) * (
+        2.0 * math.pi / samples
+    )
+    turn = jnp.concatenate([jnp.cos(turn_angle), jnp.sin(turn_angle)], axis=1)
+    angular = (bins.astype(jnp.float32) * (2.0 * math.pi / samples))[None, :]
+    lag_table = lag_weights(samples, first_bin, NF, NLAG).T
+    channel_ids = quarter * channels + me * own + jnp.arange(own, dtype=jnp.int32)
+    alive = (channel_ids[:, None] < counts[None, :]).astype(jnp.float32)
+    live = jnp.broadcast_to(alive[:, :, None], (own, NBLOCK, LANES))
+
+    stats = pl.pallas_call(
+        functools.partial(stats_kernel, own, cols),
+        out_shape=jax.ShapeDtypeStruct((shards * rows, 2, LANES), jnp.float32),
+        in_specs=[VMEM] * 7,
+        out_specs=VMEM,
+        scratch_shapes=[
+            pltpu.VMEM((shards * own * NBLOCK, 2 * NF), jnp.float32),
+            pltpu.VMEM((own * NBLOCK, NF), jnp.float32),
+            pltpu.VMEM((own * NBLOCK, NF), jnp.float32),
+            pltpu.VMEM((2 * own * REACH * NBLOCK, NF), jnp.bfloat16),
+        ],
+        name="stats",
+    )(received, table_high, table_low, turn, angular, lag_table, live)
+    gathered = lax.all_to_all(stats, ("pair", "row"), split_axis=0, concat_axis=0, tiled=True)
+    gathered = gathered.reshape(shards, rows, 2, LANES)
+    return pl.pallas_call(
+        functools.partial(solve_kernel, own, float(NBLOCK * CB)),
+        out_shape=jax.ShapeDtypeStruct((1, channels), jnp.float32),
+        in_specs=[VMEM, VMEM],
+        out_specs=VMEM,
+        scratch_shapes=[pltpu.VMEM((NBLOCK, NBLOCK, LANES), jnp.float32)],
+        name="solve",
+    )(gathered, jnp.broadcast_to(damping[None, :], (NBLOCK, LANES)))
+
+
+def body(records, offsets, counts, damping):
+    shards = lax.axis_size("pair")
+    channels, length, nblock = records.shape
+    own = channels // shards
+    whole = own * shards == channels and own * REACH * NBLOCK == LANES
+    if shards == NBLOCK and nblock == NBLOCK and whole and length % LANES == 0:
+        return per_device(records, offsets, counts, damping)
+    return per_device_general(records, offsets, counts, damping)
+
+
 def solution(mesh):
     return jax.shard_map(
-        per_device,
+        body,
         mesh=mesh,
         in_specs=(P("row", "pair", None), P("pair", "row"), P(), P()),
         out_specs=P("pair", "row"),

time: 172 us -> 41 us (0.24)
  blocking collectives: 73.1 us -> 0 us
  other arithmetic: 60.2 us -> 10.8 us
  local copies, waits for them, and re-layouts: 9.21 us -> 1.32 us
  Pallas kernels: 0 us -> 7.8 us
  matrix products: 6.83 us -> 0 us
  starting transfers between devices: 7.28 us -> 13.3 us
  loops' own time: 5.79 us -> 0 us
    psum x2 -> x0, blocking collectives: 41.5 us -> none  [the longest x1 35.2 us: per_device(): hessian, gradient = lax.psum((hessian, gradient), 'pair')]
    all_gather x1 -> x0, blocking collectives: 31.6 us -> none  [per_device(): segment = lax.all_gather(own_spec[None], 'pair', axis=0, tiled=True)]
    cos x8 -> x1, other arithmetic: 33.2 us -> 4.09 us  [band_table(): return jnp.concatenate([jnp.cos(angles), jnp.sin(angles)], axis=1)]
    another operation x11 -> x0, other arithmetic: 24.6 us -> none  [the longest x4 23.6 us: per_device(): factor = jnp.linalg.cholesky(system)]
    pallas_call x0 -> x3, Pallas kernels: none -> 7.8 us  [the longest x1 3.65 us: per_device(): pl.pallas_call(functools.partial(stats_kernel, own, cols), out_shape=jax....]
    dot_general x17 -> x0, matrix products: 6.83 us -> none  [the longest x8 2.3 us: accumulate(): jnp.dot(segment, table_high, preferred_element_type=jnp.float32)]
    all_to_all x1 -> x2, starting transfers between devices: 7.28 us -> 13.3 us  [the longest x1 7.29 us: per_device(): lax.all_to_all(payload, 'pair', split_axis=0, concat_axis=0, tiled=True)]
    dynamic_slice x9 -> x0, local copies, waits for them, and re-layouts: 6.02 us -> none  [the longest x8 5.37 us: per_device(): lax.scan(accumulate, jnp.zeros((channels, 2 * NF), jnp.float32), jnp.aran...]
  transfers between devices with their start and end apart: 1 -> 2, of which waited for: 1 -> 1; matrix products, arithmetic and copies ran while one was open for 0% -> 27% of each run, Pallas kernels for 0% -> 0%
where the time goes in v1:
time: 41 us; the launch traced here: 40.6 us
  starting transfers between devices  13.3 us (32%)
  other arithmetic  10.8 us (26%)
  Pallas kernels  7.8 us (19%)
  waiting for transfers between devices  6.61 us (16%)
  local copies, waits for them, and re-layouts  1.32 us (3%)
  between operations  0.7 us (2%)
    all_to_all x1, starting transfers between devices, per_device(): lax.all_to_all(payload, 'pair', split_axis=0, concat_axis=0, tiled=True)  7.29 us
    all_to_all x1, waiting for transfers between devices, per_device(): lax.all_to_all(stats, ('pair', 'row'), split_axis=0, concat_axis=0, tiled...  6.61 us
    all_to_all x1, starting transfers between devices, per_device(): lax.all_to_all(stats, ('pair', 'row'), split_axis=0, concat_axis=0, tiled...  6.05 us
    cos x1, other arithmetic, band_table(): return jnp.concatenate([jnp.cos(angles), jnp.sin(angles)], axis=1)  4.09 us
    pallas_call x1, Pallas kernels, per_device(): pl.pallas_call(functools.partial(stats_kernel, own, cols), out_shape=jax....  3.65 us
    convert_element_type x1, other arithmetic, lag_weights(): return (-2.0 * weight[:, None] * jnp.sin(angles)).astype(jnp.bfloat16)  2.77 us
    pallas_call x1, Pallas kernels, per_device(): pl.pallas_call(functools.partial(pack_kernel, own, cols), out_shape=jax.S...  2.57 us
    pallas_call x1, Pallas kernels, per_device(): pl.pallas_call(functools.partial(solve_kernel, own, float(NBLOCK * CB)),...  1.59 us
  transfers between devices with their start and end apart: 2, of which 1 were waited for; matrix products, arithmetic and copies ran while one was open for 27% of the time, Pallas kernels for 0%

profile of v1, /device:TPU:0, one launch (start us, length us, event | category | flops | bytes accessed | tf_op | source)
XLA Modules:
  0.0 40.6 jit_solution(15734089596762511914)
XLA Ops:
  0.0 2.6 %pack.1 = bf16[8,17,8,128]{3,2,1,0:T(8,128)(2,1)} custom-call(bf16[32,8,512]{2,1,0:T(8,128)(2,1)} %bitcast.4, f32[1,32]{1,0:T(1,128)} %off_ref.1), custom_call_target="tpu_custom_call" | custom-call | tf_op jit(solution)/shard_map/pack/pallas_call | solution.py:336
  2.6 7.3 %all-to-all-start = ((bf16[8,17,8,128]{3,2,1,0:T(8,128)(2,1)}), bf16[8,17,8,128]{3,2,1,0:T(8,128)(2,1)S(1)}, u32[]{:S(2)}, u32[]{:S(2)}) async-start(bf16[8,17,8,128]{3,2,1,0:T(8,128)(2,1)} %pack.1), calls=%async_computation | async-start | bytes 557056 | tf_op jit(solution)/shard_map/all_to_all | solution.py:347
  9.9 4.1 %fusion.15 = (f32[512,512]{1,0:T(8,128)S(1)}, f32[512,512]{1,0:T(8,128)S(1)}) fusion(s32[512]{0:T(512)S(1)} %iota_add_fusion), kind=kLoop, calls=%fused_computation.25 | loop fusion | flops 3670016 | bytes 2099200 | tf_op jit(solution)/shard_map/cos | solution.py:21
  14.0 1.4 %fusion.low_ref = bf16[512,1024]{1,0:T(8,128)(2,1)} fusion(f32[512,512]{1,0:T(8,128)S(1)} %get-tuple-element.8, f32[512,512]{1,0:T(8,128)S(1)} %get-tuple-element.7), kind=kLoop, calls=%fused_computation.1 | loop fusion | flops 2097152 | bytes 3145728 | tf_op jit(solution)/shard_map/convert_element_type | solution.py:351
  15.3 0.0 copy-start.2
  15.3 1.1 %fusion.1.high_ref = bf16[512,1024]{1,0:T(8,128)(2,1)} fusion(f32[512,512]{1,0:T(8,128)S(1)} %get-tuple-element.8, f32[512,512]{1,0:T(8,128)S(1)} %get-tuple-element.7), kind=kLoop, calls=%fused_computation.3 | loop fusion | flops 2097152 | bytes 3145728 | tf_op jit(solution)/shard_map/convert_element_type | solution.py:350
  16.5 0.6 %convert_multiply_fusion.ang_ref = f32[1,512]{1,0:T(1,128)} fusion(), kind=kLoop, calls=%fused_computation.38 | loop fusion | flops 1536 | bytes 2048 | tf_op jit(solution)/shard_map/mul | solution.py:358
  17.1 0.2 fusion.20
  17.2 0.6 %pad_maximum_fusion.1.turn_ref = f32[8,1024]{1,0:T(8,128)} fusion(f32[8,512]{1,0:T(8,128)S(1)} %get-tuple-element.6, f32[8,512]{1,0:T(8,128)S(1)} %get-tuple-element.5), kind=kLoop, calls=%fused_computation.26 | loop fusion | flops 8192 | bytes 65536 | tf_op jit(solution)/shard_map/concatenate | solution.py:357
  17.9 0.0 copy-done.2
  17.9 0.1 compare_convert_fusion
  17.9 2.8 %fusion.12.lag_ref = bf16[256,512]{1,0:T(8,128)(2,1)} fusion(s32[256]{0:T(256)S(1)} %iota_add_fusion.1, s32[512]{0:T(512)S(1)} %iota_add_fusion, f32[512]{0:T(512)S(1)} %multiply_multiply_fusion), kind=kLoop, calls=%fused_computation.22 | loop fusion | flops 2097152 | bytes 267264 | tf_op jit(solution)/shard_map/convert_element_type | solution.py:31
  20.7 0.0 all-to-all-done.x_ref
  20.7 0.0 copy-start
  20.7 0.7 %broadcast_in_dim.6.live_ref = f32[4,8,128]{2,1,0:T(8,128)} broadcast(f32[4,8]{1,0:T(4,128)S(1)} %compare_convert_fusion), dimensions={0,1} | broadcast | bytes 16512 | tf_op jit(solution)/shard_map/broadcast_in_dim | solution.py:362
  21.4 0.0 copy-done
  21.4 3.6 %stats.1 = f32[32,2,128]{2,1,0:T(2,128)} custom-call(bf16[8,17,8,128]{3,2,1,0:T(8,128)(2,1)} %copy-done, bf16[512,1024]{1,0:T(8,128)(2,1)} %fusion.1.high_ref, bf16[512,1024]{1,0:T(8,128)(2,1)} %fusion.low_ref, f32[8,1024]{1,0:T(8,128)} %pad_maximum_fusion.1.turn_ref, f32[1,512]{1,0:T(1,128)} %convert_multiply_fusion.ang_ref, ...), custom_call_target="tpu_custom_call" | custom-call | tf_op jit(solution)/shard_map/stats/pallas_call | solution.py:364
  25.1 6.0 %all-to-all-start.1 = ((f32[32,2,128]{2,1,0:T(2,128)}), f32[32,2,128]{2,1,0:T(2,128)S(1)}, u32[]{:S(2)}, u32[]{:S(2)}) async-start(f32[32,2,128]{2,1,0:T(2,128)} %stats.1), calls=%async_computation.1 | async-start | bytes 65536 | tf_op jit(solution)/shard_map/all_to_all | solution.py:377
  31.8 6.6 %all-to-all-done.1 = f32[32,2,128]{2,1,0:T(2,128)S(1)} async-done(((f32[32,2,128]{2,1,0:T(2,128)}), f32[32,2,128]{2,1,0:T(2,128)S(1)}, u32[]{:S(2)}, u32[]{:S(2)}) %all-to-all-start.1) | async-done | bytes 32800 | tf_op jit(solution)/shard_map/all_to_all | solution.py:377
  38.4 0.0 copy-start.1
  38.4 0.6 %broadcast_in_dim.8.damp_ref = f32[8,128]{1,0:T(8,128)} broadcast(f32[]{:T(128)} %bitcast.3), dimensions={} | broadcast | bytes 4100 | tf_op jit(solution)/shard_map/broadcast_in_dim | solution.py:386
  39.0 0.0 copy-done.1
  39.0 1.6 %solve.1 = f32[1,32]{1,0:T(1,128)} custom-call(f32[8,4,2,128]{3,2,1,0:T(2,128)} %bitcast.5, f32[8,128]{1,0:T(8,128)} %broadcast_in_dim.8.damp_ref), custom_call_target="tpu_custom_call" | custom-call | tf_op jit(solution)/shard_map/solve/pallas_call | solution.py:379
  (5 shorter events, 0.1 us)
Async XLA Ops:
  2.6 18.1 %all-to-all-start = ((bf16[8,17,8,128]{3,2,1,0:T(8,128)(2,1)}), bf16[8,17,8,128]{3,2,1,0:T(8,128)(2,1)S(1)}, u32[]{:S(2)}, u32[]{:S(2)}) async-start(bf16[8,17,8,128]{3,2,1,0:T(8,128)(2,1)} %pack.1), calls=%async_computation | async-start | bytes 557056 | tf_op jit(solution)/shard_map/all_to_all | solution.py:347
  15.3 2.5 %copy-start.2 = (s32[8]{0:T(128)S(1)}, s32[8]{0:T(128)}, u32[]{:S(2)}) copy-start(s32[8]{0:T(128)} %param.6) | copy-start | bytes 100
  20.7 0.7 %copy-start = (bf16[8,17,8,128]{3,2,1,0:T(8,128)(2,1)}, bf16[8,17,8,128]{3,2,1,0:T(8,128)(2,1)S(1)}, u32[]{:S(2)}) copy-start(bf16[8,17,8,128]{3,2,1,0:T(8,128)(2,1)S(1)} %all-to-all-done.x_ref) | copy-start | bytes 835588
  25.1 13.3 %all-to-all-start.1 = ((f32[32,2,128]{2,1,0:T(2,128)}), f32[32,2,128]{2,1,0:T(2,128)S(1)}, u32[]{:S(2)}, u32[]{:S(2)}) async-start(f32[32,2,128]{2,1,0:T(2,128)} %stats.1), calls=%async_computation.1 | async-start | bytes 65536 | tf_op jit(solution)/shard_map/all_to_all | solution.py:377
  38.4 0.6 %copy-start.1 = (f32[32,2,128]{2,1,0:T(2,128)}, f32[32,2,128]{2,1,0:T(2,128)S(1)}, u32[]{:S(2)}) copy-start(f32[32,2,128]{2,1,0:T(2,128)S(1)} %all-to-all-done.1) | copy-start | bytes 98308

commit v2 on v1

--- a/solution.py
+++ b/solution.py
@@ -124,19 +124,19 @@
 ANY = pl.BlockSpec(memory_space=pl.ANY)
 
 
-def pack_kernel(own, cols, rec_ref, off_ref, out_ref, wide, sems):
-    ndest = out_ref.shape[0]
-    copies = []
-    for dest in range(ndest):
-        for col in range(cols):
-            copies.append(
-                pltpu.make_async_copy(
-                    rec_ref.at[pl.ds(dest * own, own), :, pl.ds(col * LANES, LANES)],
-                    out_ref.at[dest, pl.ds(col * own, own)],
-                    sems.at[dest, col],
-                )
-            )
-            copies[-1].start()
+def pack_kernel(rec_ref, off_ref, out_ref, wide, sems):
+    ndest, own, _, length = rec_ref.shape
+    cols = length // LANES
+    copies = [
+        pltpu.make_async_copy(
+            rec_ref.at[:, :, :, pl.ds(col * LANES, LANES)],
+            out_ref.at[:, pl.ds(col * own, own)],
+            sems.at[col],
+        )
+        for col in range(cols)
+    ]
+    for copy in copies:
+        copy.start()
     channels = off_ref.shape[1]
     wide[...] = jnp.zeros_like(wide)
     wide[:, :channels] = jnp.broadcast_to(off_ref[...], (NBLOCK, channels))
@@ -163,8 +163,86 @@
     return sine * angle, cosine
 
 
+def unit_circle(phase, samples):
+    phase = lax.bitwise_and(phase, samples - 1)
+    phase = jnp.where(phase >= samples // 2, phase - samples, phase)
+    sine, cosine = sin_cos(phase.astype(jnp.float32) * jnp.float32(math.pi / samples))
+    return 1.0 - 2.0 * sine * sine, 2.0 * sine * cosine
+
+
+def table_kernel(
+    order, samples, counts_ref, damp_ref,
+    high_ref, low_ref, turn_ref, ang_ref, lag_ref, live_ref, wide_ref, coarse,
+):
+    shards = len(order)
+    length = samples // shards
+    own = live_ref.shape[0]
+    rows = 16
+    first_bin = samples // 8
+
+    def bins(height):
+        return first_bin + lax.broadcasted_iota(jnp.int32, (height, NF), 1)
+
+    def ids(height):
+        return lax.broadcasted_iota(jnp.int32, (height, NF), 0)
+
+    fine_cos, fine_sin = unit_circle(ids(rows) * bins(rows), samples)
+    height = length // rows
+    wide_cos, wide_sin = unit_circle(ids(height) * rows * bins(height), samples)
+    coarse[pl.ds(0, height), :NF] = wide_cos
+    coarse[pl.ds(0, height), NF:] = wide_sin
+
+    @pl.loop(0, height)
+    def _(step):
+        row_cos = coarse[pl.ds(step, 1), :NF]
+        row_sin = coarse[pl.ds(step, 1), NF:]
+        at = pl.ds(pl.multiple_of(step * rows, rows), rows)
+        for part, value in enumerate(
+            (row_cos * fine_cos - row_sin * fine_sin, row_sin * fine_cos + row_cos * fine_sin)
+        ):
+            cut = pl.ds(part * NF, NF)
+            high = value.astype(jnp.bfloat16)
+            high_ref[at, cut] = high
+            low_ref[at, cut] = (value - high.astype(jnp.float32)).astype(jnp.bfloat16)
+
+    lags = NLAG // rows
+    wide_cos, wide_sin = unit_circle((ids(lags) * rows + 1) * bins(lags), samples)
+    coarse[pl.ds(0, lags), :NF] = wide_cos
+    coarse[pl.ds(0, lags), NF:] = wide_sin
+    centre = (lax.broadcasted_iota(jnp.int32, (1, NF), 1).astype(jnp.float32) + 0.5) * (
+        math.pi / NF
+    )
+    _, weight = sin_cos(centre - jnp.float32(math.pi / 2))
+    factor = -2.0 * (weight * weight)
+    lag_cos = fine_cos * factor
+    lag_sin = fine_sin * factor
+
+    @pl.loop(0, lags)
+    def _(step):
+        row_cos = coarse[pl.ds(step, 1), :NF]
+        row_sin = coarse[pl.ds(step, 1), NF:]
+        at = pl.ds(pl.multiple_of(step * rows, rows), rows)
+        lag_ref[at, :] = (row_sin * lag_cos + row_cos * lag_sin).astype(jnp.bfloat16)
+
+    turn_cos, turn_sin = unit_circle(ids(shards) * length * bins(shards), samples)
+    turn_ref[:, :NF] = turn_cos
+    turn_ref[:, NF:] = turn_sin
+    ang_ref[...] = bins(NBLOCK).astype(jnp.float32) * jnp.float32(2.0 * math.pi / samples)
+
+    me = lax.axis_index("pair")
+    slot = jnp.where(me == order[0], 0, jnp.where(me < order[0], me + 1, me))
+    first_channel = (lax.axis_index("row") * shards + slot) * own
+    block_ids = lax.broadcasted_iota(jnp.int32, (NBLOCK, LANES), 0)
+    limit = jnp.zeros((NBLOCK, LANES), jnp.int32)
+    for block in range(NBLOCK):
+        limit = jnp.where(block_ids == block, counts_ref[block], limit)
+    for c in range(own):
+        live_ref[c] = (limit > first_channel + c).astype(jnp.float32)
+    wide_ref[...] = jnp.full((NBLOCK, LANES), damp_ref[0], jnp.float32)
+
+
 def stats_kernel(
-    own, cols, x_ref, high_ref, low_ref, turn_ref, ang_ref, lag_ref, live_ref, out_ref,
+    order, own, cols, x_ref, high_ref, low_ref, turn_ref, ang_ref, lag_ref, live_ref, out_ref,
     spectrum, re_ref, im_ref, stacked,
 ):
     shards = x_ref.shape[0]
@@ -193,7 +271,7 @@
     pieces = jnp.zeros((NBLOCK, LANES), jnp.float32)
     for shard in range(shards):
         pieces = jnp.where(
-            block_ids == shard, x_ref[shard, cols * own].astype(jnp.float32), pieces
+            block_ids == order[shard], x_ref[shard, cols * own].astype(jnp.float32), pieces
         )
     channels = own * shards
     shift = (pieces + pltpu.roll(pieces, LANES - channels, 1)) + pltpu.roll(
@@ -203,11 +281,14 @@
     for col in range(NF // LANES):
         at = pl.ds(col * LANES, LANES)
         at_sine = pl.ds(NF + col * LANES, LANES)
-        cosine_part = spectrum[pl.ds(0, rows), at]
-        sine_part = spectrum[pl.ds(0, rows), at_sine]
-        for shard in range(1, shards):
-            turn_cos = turn_ref[pl.ds(shard, 1), at]
-            turn_sin = turn_ref[pl.ds(shard, 1), at_sine]
+        home = order.index(0)
+        cosine_part = spectrum[pl.ds(home * rows, rows), at]
+        sine_part = spectrum[pl.ds(home * rows, rows), at_sine]
+        for shard in range(shards):
+            if shard == home:
+                continue
+            turn_cos = turn_ref[pl.ds(order[shard], 1), at]
+            turn_sin = turn_ref[pl.ds(order[shard], 1), at_sine]
             part_cos = spectrum[pl.ds(shard * rows, rows), at]
             part_sin = spectrum[pl.ds(shard * rows, rows), at_sine]
             cosine_part += turn_cos * part_cos - turn_sin * part_sin
@@ -251,7 +332,7 @@
     out_ref[...] = jnp.broadcast_to(both[None], out_ref.shape)
 
 
-def solve_kernel(own, total, got_ref, damp_ref, out_ref, steps):
+def solve_kernel(order, own, total, got_ref, damp_ref, out_ref, steps):
     shards = got_ref.shape[0]
     quarter = lax.axis_index("row")
     me = lax.axis_index("pair")
@@ -267,10 +348,10 @@
     level = jnp.sum(jnp.where(inner, 2.0 * summed, summed), axis=1, keepdims=True) / total
 
     squares = jnp.concatenate(
-        [got_ref[shard, quarter, 0:1, :] for shard in range(shards)], axis=0
+        [got_ref[shard, quarter, 0:1, :] for shard in order], axis=0
     )
     products = jnp.concatenate(
-        [got_ref[shard, quarter, 1:2, :] for shard in range(shards)], axis=0
+        [got_ref[shard, quarter, 1:2, :] for shard in order], axis=0
     )
 
     def entry(array, reach, block):
@@ -321,48 +402,58 @@
     out_ref[...] = jnp.sum(placed, axis=0, keepdims=True)[:, : out_ref.shape[1]]
 
 
+def room(mebibytes):
+    return pltpu.CompilerParams(vmem_limit_bytes=mebibytes << 20)
+
+
 def per_device(records, offsets, counts, damping):
     shards = lax.axis_size("pair")
     rows = lax.axis_size("row")
-    me = lax.axis_index("pair")
-    quarter = lax.axis_index("row")
     channels, length, _ = records.shape
     samples = length * shards
-    first_bin = samples // 8
     own = channels // shards
     cols = length // LANES
     tiles = own * cols + 1
-
+    lead = shards // 2
+    order = (lead, *range(lead), *range(lead + 1, shards))
+
+    by_owner = jnp.transpose(records, (0, 2, 1)).reshape(shards, own, NBLOCK, length)
     payload = pl.pallas_call(
-        functools.partial(pack_kernel, own, cols),
+        pack_kernel,
         out_shape=jax.ShapeDtypeStruct((shards, tiles, NBLOCK, LANES), jnp.bfloat16),
         in_specs=[ANY, VMEM],
         out_specs=VMEM,
         scratch_shapes=[
             pltpu.VMEM((NBLOCK, LANES), jnp.float32),
-            pltpu.SemaphoreType.DMA((shards, cols)),
+            pltpu.SemaphoreType.DMA((cols,)),
         ],
+        compiler_params=room(4),
         name="pack",
-    )(jnp.transpose(records, (0, 2, 1)), offsets)
-    received = lax.all_to_all(payload, "pair", split_axis=0, concat_axis=0, tiled=True)
-
-    table = band_table(0, length, samples, first_bin, NF)
-    table_high = table.astype(jnp.bfloat16)
-    table_low = (table - lax.reduce_precision(table, 8, 7)).astype(jnp.bfloat16)
-    turn_ids = length * jnp.arange(shards, dtype=jnp.int32)[:, None]
-    bins = first_bin + jnp.arange(NF, dtype=jnp.int32)
-    turn_angle = (turn_ids * bins[None, :] % samples).astype(jnp.float32) * (
-        2.0 * math.pi / samples
-    )
-    turn = jnp.concatenate([jnp.cos(turn_angle), jnp.sin(turn_angle)], axis=1)
-    angular = (bins.astype(jnp.float32) * (2.0 * math.pi / samples))[None, :]
-    lag_table = lag_weights(samples, first_bin, NF, NLAG).T
-    channel_ids = quarter * channels + me * own + jnp.arange(own, dtype=jnp.int32)
-    alive = (channel_ids[:, None] < counts[None, :]).astype(jnp.float32)
-    live = jnp.broadcast_to(alive[:, :, None], (own, NBLOCK, LANES))
+    )(by_owner, offsets)
+    received = lax.all_to_all(
+        payload, "pair", split_axis=0, concat_axis=0, tiled=True, axis_index_groups=[list(order)]
+    )
+
+    tables = pl.pallas_call(
+        functools.partial(table_kernel, order, samples),
+        out_shape=(
+            jax.ShapeDtypeStruct((length, 2 * NF), jnp.bfloat16),
+            jax.ShapeDtypeStruct((length, 2 * NF), jnp.bfloat16),
+            jax.ShapeDtypeStruct((shards, 2 * NF), jnp.float32),
+            jax.ShapeDtypeStruct((NBLOCK, NF), jnp.float32),
+            jax.ShapeDtypeStruct((NLAG, NF), jnp.bfloat16),
+            jax.ShapeDtypeStruct((own, NBLOCK, LANES), jnp.float32),
+            jax.ShapeDtypeStruct((NBLOCK, LANES), jnp.float32),
+        ),
+        in_specs=[pl.BlockSpec(memory_space=pltpu.SMEM)] * 2,
+        out_specs=(VMEM,) * 7,
+        scratch_shapes=[pltpu.VMEM((max(length, NLAG) // 16, 2 * NF), jnp.float32)],
+        compiler_params=room(8),
+        name="tables",
+    )(counts, damping)
 
     stats = pl.pallas_call(
-        functools.partial(stats_kernel, own, cols),
+        functools.partial(stats_kernel, order, own, cols),
         out_shape=jax.ShapeDtypeStruct((shards * rows, 2, LANES), jnp.float32),
         in_specs=[VMEM] * 7,
         out_specs=VMEM,
@@ -372,18 +463,20 @@
             pltpu.VMEM((own * NBLOCK, NF), jnp.float32),
             pltpu.VMEM((2 * own * REACH * NBLOCK, NF), jnp.bfloat16),
         ],
+        compiler_params=room(12),
         name="stats",
-    )(received, table_high, table_low, turn, angular, lag_table, live)
+    )(received, *tables[:6])
     gathered = lax.all_to_all(stats, ("pair", "row"), split_axis=0, concat_axis=0, tiled=True)
     gathered = gathered.reshape(shards, rows, 2, LANES)
     return pl.pallas_call(
-        functools.partial(solve_kernel, own, float(NBLOCK * CB)),
+        functools.partial(solve_kernel, order, own, float(NBLOCK * CB)),
         out_shape=jax.ShapeDtypeStruct((1, channels), jnp.float32),
         in_specs=[VMEM, VMEM],
         out_specs=VMEM,
         scratch_shapes=[pltpu.VMEM((NBLOCK, NBLOCK, LANES), jnp.float32)],
+        compiler_params=room(4),
         name="solve",
-    )(gathered, jnp.broadcast_to(damping[None, :], (NBLOCK, LANES)))
+    )(gathered, tables[6])
 
 
 def body(records, offsets, counts, damping):
@@ -391,7 +484,8 @@
     channels, length, nblock = records.shape
     own = channels // shards
     whole = own * shards == channels and own * REACH * NBLOCK == LANES
-    if shards == NBLOCK and nblock == NBLOCK and whole and length % LANES == 0:
+    even = length % LANES == 0 and length & (length - 1) == 0
+    if shards == NBLOCK and nblock == NBLOCK and whole and even:
         return per_device(records, offsets, counts, damping)
     return per_device_general(records, offsets, counts, damping)
 

time: 41 us -> 31.4 us (0.77)
  other arithmetic: 10.8 us -> 0 us
  blocking collectives: 0 us -> 10.7 us
  starting transfers between devices: 13.3 us -> 7.85 us
  Pallas kernels: 7.8 us -> 4.66 us
  waiting for transfers between devices: 6.61 us -> 5.5 us
    all_to_all x0 -> x1, blocking collectives: none -> 10.7 us  [per_device(): lax.all_to_all(stats, ('pair', 'row'), split_axis=0, concat_axis=0, tiled...]
    all_to_all x2 -> x1, starting transfers between devices: 13.3 us -> 7.85 us  [per_device(): lax.all_to_all(payload, 'pair', split_axis=0, concat_axis=0, tiled=True,...]
    convert_element_type x4 -> x0, other arithmetic: 5.29 us -> none  [the longest x1 2.77 us: lag_weights(): return (-2.0 * weight[:, None] * jnp.sin(angles)).astype(jnp.bfloat16)]
    cos x2 -> x0, other arithmetic: 4.24 us -> none  [the longest x1 4.09 us: band_table(): return jnp.concatenate([jnp.cos(angles), jnp.sin(angles)], axis=1)]
    pallas_call x3 -> x4, Pallas kernels: 7.8 us -> 4.66 us  [the longest x1 1.57 us: per_device(): pl.pallas_call(functools.partial(table_kernel, order, samples), out_shape...]
    unnamed x6, local copies, waits for them, and re-layouts: 0.01 us -> 1.61 us
    broadcast_in_dim x2 -> x0, local copies, waits for them, and re-layouts: 1.3 us -> none  [the longest x1 0.71 us: per_device(): live = jnp.broadcast_to(alive[:, :, None], (own, NBLOCK, LANES))]
    all_to_all x2 -> x1, waiting for transfers between devices: 6.61 us -> 5.5 us  [per_device(): lax.all_to_all(payload, 'pair', split_axis=0, concat_axis=0, tiled=True,...]
  transfers between devices with their start and end apart: 2 -> 1, of which waited for: 1 -> 1; matrix products, arithmetic and copies ran while one was open for 27% -> 0% of each run, Pallas kernels for 0% -> 5%
where the time goes in v2:
time: 31.4 us; the launch traced here: 31.1 us
  blocking collectives  10.7 us (34%)
  starting transfers between devices  7.85 us (25%)
  waiting for transfers between devices  5.5 us (18%)
  Pallas kernels  4.66 us (15%)
  local copies, waits for them, and re-layouts  1.61 us (5%)
  between operations  0.7 us (2%)
    all_to_all x1, blocking collectives, per_device(): lax.all_to_all(stats, ('pair', 'row'), split_axis=0, concat_axis=0, tiled...  10.7 us
    all_to_all x1, starting transfers between devices, per_device(): lax.all_to_all(payload, 'pair', split_axis=0, concat_axis=0, tiled=True,...  7.85 us
    all_to_all x1, waiting for transfers between devices, per_device(): lax.all_to_all(payload, 'pair', split_axis=0, concat_axis=0, tiled=True,...  5.5 us
    unnamed x6, local copies, waits for them, and re-layouts  1.61 us
    pallas_call x1, Pallas kernels, per_device(): pl.pallas_call(functools.partial(table_kernel, order, samples), out_shape...  1.57 us
    pallas_call x1, Pallas kernels, per_device(): pl.pallas_call(functools.partial(stats_kernel, order, own, cols), out_sha...  1.31 us
    pallas_call x1, Pallas kernels, per_device(): pl.pallas_call(pack_kernel, out_shape=jax.ShapeDtypeStruct((shards, tiles...  0.95 us
    pallas_call x1, Pallas kernels, per_device(): pl.pallas_call(functools.partial(solve_kernel, order, own, float(NBLOCK *...  0.83 us
  transfers between devices with their start and end apart: 1, of which 1 were waited for; matrix products, arithmetic and copies ran while one was open for 0% of the time, Pallas kernels for 5%

profile of v2, /device:TPU:0, one launch (start us, length us, event | category | flops | bytes accessed | tf_op | source)
XLA Modules:
  0.0 31.1 jit_solution(7117894694781308395)
XLA Ops:
  0.0 0.0 copy-start.1
  0.0 0.7 %copy-done.1 = f32[1,32]{1,0:T(1,128)S(1)} copy-done((f32[1,32]{1,0:T(1,128)S(1)}, f32[1,32]{1,0:T(1,128)}, u32[]{:S(2)}) %copy-start.1) | copy-done | bytes 152
  0.7 0.0 copy-start
  0.7 0.9 %copy-done = bf16[32,512,8]{1,2,0:T(8,128)(2,1)S(1)} copy-done((bf16[32,512,8]{1,2,0:T(8,128)(2,1)S(1)}, bf16[32,512,8]{1,2,0:T(8,128)(2,1)}, u32[]{:S(2)}) %copy-start) | copy-done | bytes 262168
  1.6 0.9 %pack.1 = bf16[8,17,8,128]{3,2,1,0:T(8,128)(2,1)} custom-call(bf16[8,4,8,512]{3,2,1,0:T(8,128)(2,1)S(1)} %bitcast.4, f32[1,32]{1,0:T(1,128)S(1)} %copy-done.1), custom_call_target="tpu_custom_call" | custom-call | tf_op jit(solution)/shard_map/pack/pallas_call | solution.py:421
  2.6 7.9 %all-to-all-start = ((bf16[8,17,8,128]{3,2,1,0:T(8,128)(2,1)}), bf16[8,17,8,128]{3,2,1,0:T(8,128)(2,1)S(1)}, u32[]{:S(2)}, u32[]{:S(2)}) async-start(bf16[8,17,8,128]{3,2,1,0:T(8,128)(2,1)} %pack.1), calls=%async_computation | async-start | bytes 557056 | tf_op jit(solution)/shard_map/all_to_all | solution.py:433
  10.4 0.0 copy-start.2
  11.1 0.0 copy-done.2
  11.1 1.6 %tables.1 = (bf16[512,1024]{1,0:T(8,128)(2,1)S(1)}, bf16[512,1024]{1,0:T(8,128)(2,1)S(1)}, f32[8,1024]{1,0:T(8,128)S(1)}, f32[8,512]{1,0:T(8,128)S(1)}, bf16[256...) custom-call(s32[8]{0:T(128)S(1)} %copy-done.2, f32[1]{0:T(128)S(6)} %copy.5.damp_ref), custom_call_target="tpu_custom_call" | custom-call | tf_op jit(solution)/shard_map/tables/pallas_call | solution.py:437
  12.7 5.5 %all-to-all-done.x_ref = bf16[8,17,8,128]{3,2,1,0:T(8,128)(2,1)S(1)} async-done(((bf16[8,17,8,128]{3,2,1,0:T(8,128)(2,1)}), bf16[8,17,8,128]{3,2,1,0:T(8,128)(2,1)S(1)}, u32[]{:S(2)}, u32[]{:S(2)}) %all-to-all-start) | async-done | bytes 278560 | tf_op jit(solution)/shard_map/all_to_all | solution.py:433
  18.2 1.3 %stats.1 = f32[32,2,128]{2,1,0:T(2,128)S(1)} custom-call(bf16[8,17,8,128]{3,2,1,0:T(8,128)(2,1)S(1)} %all-to-all-done.x_ref, bf16[512,1024]{1,0:T(8,128)(2,1)S(1)} %get-tuple-element.12.high_ref, bf16[512,1024]{1,0:T(8,128)(2,1)S(1)} %get-tuple-element.13.low_ref, f32[8,1024]{1,0:T(8,128)S(1)} %get-tuple-element.14.turn_ref, ...), custom_call_target="tpu_custom_call" | custom-call | tf_op jit(solution)/shard_map/stats/pallas_call | solution.py:455
  19.5 10.7 %all_to_all.10 = f32[32,2,128]{2,1,0:T(2,128)S(1)} all-to-all(f32[32,2,128]{2,1,0:T(2,128)S(1)} %stats.1), channel_id=1, replica_groups=mesh['pair'=8,'row'=4] {'pair','row'}, dimensions={0} | all-to-all | bytes 65536 | tf_op jit(solution)/shard_map/all_to_all | solution.py:469
  30.2 0.8 %solve.1 = f32[1,32]{1,0:T(1,128)} custom-call(f32[8,4,2,128]{3,2,1,0:T(2,128)S(1)} %bitcast.5, f32[8,128]{1,0:T(8,128)S(1)} %get-tuple-element.18.damp_ref), custom_call_target="tpu_custom_call" | custom-call | tf_op jit(solution)/shard_map/solve/pallas_call | solution.py:471
Async XLA Ops:
  0.0 0.7 %copy-start.1 = (f32[1,32]{1,0:T(1,128)S(1)}, f32[1,32]{1,0:T(1,128)}, u32[]{:S(2)}) copy-start(f32[1,32]{1,0:T(1,128)} %off_ref.1) | copy-start | bytes 388
  0.7 0.9 %copy-start = (bf16[32,512,8]{1,2,0:T(8,128)(2,1)S(1)}, bf16[32,512,8]{1,2,0:T(8,128)(2,1)}, u32[]{:S(2)}) copy-start(bf16[32,512,8]{1,2,0:T(8,128)(2,1)} %param.4) | copy-start | bytes 786436
  2.6 15.6 %all-to-all-start = ((bf16[8,17,8,128]{3,2,1,0:T(8,128)(2,1)}), bf16[8,17,8,128]{3,2,1,0:T(8,128)(2,1)S(1)}, u32[]{:S(2)}, u32[]{:S(2)}) async-start(bf16[8,17,8,128]{3,2,1,0:T(8,128)(2,1)} %pack.1), calls=%async_computation | async-start | bytes 557056 | tf_op jit(solution)/shard_map/all_to_all | solution.py:433
  10.4 0.7 %copy-start.2 = (s32[8]{0:T(128)S(1)}, s32[8]{0:T(128)}, u32[]{:S(2)}) copy-start(s32[8]{0:T(128)} %counts_ref.1) | copy-start | bytes 100

commit v3 on v2

--- a/solution.py
+++ b/solution.py
@@ -121,24 +121,30 @@
 NBLOCK = 8
 REACH = NBLOCK // 2
 VMEM = pl.BlockSpec(memory_space=pltpu.VMEM)
-ANY = pl.BlockSpec(memory_space=pl.ANY)
-
-
-def pack_kernel(rec_ref, off_ref, out_ref, wide, sems):
-    ndest, own, _, length = rec_ref.shape
+HBM = pl.BlockSpec(memory_space=pltpu.HBM)
+
+
+def pack_kernel(rec_hbm, off_hbm, out_hbm, held, off_ref, wide, sems, done):
+    ndest, own, _, length = rec_hbm.shape
     cols = length // LANES
-    copies = [
+    parts = [pl.ds(col * own, own) for col in range(cols)] + [pl.ds(cols * own, 1)]
+    leaving = [
+        pltpu.make_async_copy(held.at[:, part], out_hbm.at[:, part], done.at[index])
+        for index, part in enumerate(parts)
+    ]
+    offsets = pltpu.make_async_copy(off_hbm, off_ref, sems.at[cols])
+    offsets.start()
+    arriving = [
         pltpu.make_async_copy(
-            rec_ref.at[:, :, :, pl.ds(col * LANES, LANES)],
-            out_ref.at[:, pl.ds(col * own, own)],
-            sems.at[col],
+            rec_hbm.at[:, :, :, pl.ds(col * LANES, LANES)], held.at[:, parts[col]], sems.at[col]
         )
         for col in range(cols)
     ]
-    for copy in copies:
+    for copy in arriving:
         copy.start()
     channels = off_ref.shape[1]
     wide[...] = jnp.zeros_like(wide)
+    offsets.wait()
     wide[:, :channels] = jnp.broadcast_to(off_ref[...], (NBLOCK, channels))
     value = wide[...]
     high = value.astype(jnp.bfloat16).astype(jnp.float32)
@@ -147,8 +153,12 @@
     pieces = high + pltpu.roll(middle, channels, 1) + pltpu.roll(low, 2 * channels, 1)
     for dest in range(ndest):
         tile = pieces if dest == 0 else pltpu.roll(pieces, LANES - dest * own, 1)
-        out_ref[dest, cols * own] = tile.astype(jnp.bfloat16)
-    for copy in copies:
+        held[dest, cols * own] = tile.astype(jnp.bfloat16)
+    leaving[cols].start()
+    for copy, onward in zip(arriving, leaving):
+        copy.wait()
+        onward.start()
+    for copy in leaving:
         copy.wait()
 
 
@@ -421,13 +431,15 @@
     payload = pl.pallas_call(
         pack_kernel,
         out_shape=jax.ShapeDtypeStruct((shards, tiles, NBLOCK, LANES), jnp.bfloat16),
-        in_specs=[ANY, VMEM],
-        out_specs=VMEM,
+        in_specs=[HBM, HBM],
+        out_specs=HBM,
         scratch_shapes=[
+            pltpu.VMEM((shards, tiles, NBLOCK, LANES), jnp.bfloat16),
+            pltpu.VMEM((1, channels), jnp.float32),
             pltpu.VMEM((NBLOCK, LANES), jnp.float32),
-            pltpu.SemaphoreType.DMA((cols,)),
+            pltpu.SemaphoreType.DMA((cols + 1,)),
+            pltpu.SemaphoreType.DMA((cols + 1,)),
         ],
-        compiler_params=room(4),
         name="pack",
     )(by_owner, offsets)
     received = lax.all_to_all(

time: 31.4 us -> 30.5 us (0.971)
  local copies, waits for them, and re-layouts: 1.61 us -> 0.01 us
  Pallas kernels: 4.66 us -> 5.41 us
    unnamed x6 -> x2, local copies, waits for them, and re-layouts: 1.61 us -> 0.01 us
    pallas_call x1, Pallas kernels: 0.95 us -> 1.7 us  [per_device(): pl.pallas_call(pack_kernel, out_shape=jax.ShapeDtypeStruct((shards, tiles...]
where the time goes in v3:
time: 30.5 us; the launch traced here: 30.2 us
  blocking collectives  10.8 us (35%)
  starting transfers between devices  7.85 us (26%)
  waiting for transfers between devices  5.5 us (18%)
  Pallas kernels  5.41 us (18%)
  between operations  0.7 us (2%)
    all_to_all x1, blocking collectives, per_device(): lax.all_to_all(stats, ('pair', 'row'), split_axis=0, concat_axis=0, tiled...  10.8 us
    all_to_all x1, starting transfers between devices, per_device(): lax.all_to_all(payload, 'pair', split_axis=0, concat_axis=0, tiled=True,...  7.85 us
    all_to_all x1, waiting for transfers between devices, per_device(): lax.all_to_all(payload, 'pair', split_axis=0, concat_axis=0, tiled=True,...  5.5 us
    pallas_call x1, Pallas kernels, per_device(): pl.pallas_call(pack_kernel, out_shape=jax.ShapeDtypeStruct((shards, tiles...  1.7 us
    pallas_call x1, Pallas kernels, per_device(): pl.pallas_call(functools.partial(table_kernel, order, samples), out_shape...  1.57 us
    pallas_call x1, Pallas kernels, per_device(): pl.pallas_call(functools.partial(stats_kernel, order, own, cols), out_sha...  1.31 us
    pallas_call x1, Pallas kernels, per_device(): pl.pallas_call(functools.partial(solve_kernel, order, own, float(NBLOCK *...  0.83 us
  transfers between devices with their start and end apart: 1, of which 1 were waited for; matrix products, arithmetic and copies ran while one was open for 0% of the time, Pallas kernels for 5%

profile of v3, /device:TPU:0, one launch (start us, length us, event | category | flops | bytes accessed | tf_op | source)
XLA Modules:
  0.0 30.2 jit_solution(11137118620538416878)
XLA Ops:
  0.0 1.7 %pack.1 = bf16[8,17,8,128]{3,2,1,0:T(8,128)(2,1)} custom-call(bf16[8,4,8,512]{3,2,1,0:T(8,128)(2,1)} %bitcast.5, f32[1,32]{1,0:T(1,128)} %off_hbm.1), custom_call_target="tpu_custom_call" | custom-call | tf_op jit(solution)/shard_map/pack/pallas_call | solution.py:431
  1.7 7.9 %all-to-all-start = ((bf16[8,17,8,128]{3,2,1,0:T(8,128)(2,1)}), bf16[8,17,8,128]{3,2,1,0:T(8,128)(2,1)S(1)}, u32[]{:S(2)}, u32[]{:S(2)}) async-start(bf16[8,17,8,128]{3,2,1,0:T(8,128)(2,1)} %pack.1), calls=%async_computation | async-start | bytes 557056 | tf_op jit(solution)/shard_map/all_to_all | solution.py:445
  9.6 0.0 copy-start
  10.2 0.0 copy-done
  10.2 1.6 %tables.1 = (bf16[512,1024]{1,0:T(8,128)(2,1)S(1)}, bf16[512,1024]{1,0:T(8,128)(2,1)S(1)}, f32[8,1024]{1,0:T(8,128)S(1)}, f32[8,512]{1,0:T(8,128)S(1)}, bf16[256...) custom-call(s32[8]{0:T(128)S(1)} %copy-done, f32[1]{0:T(128)S(6)} %copy.5.damp_ref), custom_call_target="tpu_custom_call" | custom-call | tf_op jit(solution)/shard_map/tables/pallas_call | solution.py:449
  11.8 5.5 %all-to-all-done.x_ref = bf16[8,17,8,128]{3,2,1,0:T(8,128)(2,1)S(1)} async-done(((bf16[8,17,8,128]{3,2,1,0:T(8,128)(2,1)}), bf16[8,17,8,128]{3,2,1,0:T(8,128)(2,1)S(1)}, u32[]{:S(2)}, u32[]{:S(2)}) %all-to-all-start) | async-done | bytes 278560 | tf_op jit(solution)/shard_map/all_to_all | solution.py:445
  17.3 1.3 %stats.1 = f32[32,2,128]{2,1,0:T(2,128)S(1)} custom-call(bf16[8,17,8,128]{3,2,1,0:T(8,128)(2,1)S(1)} %all-to-all-done.x_ref, bf16[512,1024]{1,0:T(8,128)(2,1)S(1)} %get-tuple-element.12.high_ref, bf16[512,1024]{1,0:T(8,128)(2,1)S(1)} %get-tuple-element.13.low_ref, f32[8,1024]{1,0:T(8,128)S(1)} %get-tuple-element.14.turn_ref, ...), custom_call_target="tpu_custom_call" | custom-call | tf_op jit(solution)/shard_map/stats/pallas_call | solution.py:467
  18.6 10.8 %all_to_all.10 = f32[32,2,128]{2,1,0:T(2,128)S(1)} all-to-all(f32[32,2,128]{2,1,0:T(2,128)S(1)} %stats.1), channel_id=1, replica_groups=mesh['pair'=8,'row'=4] {'pair','row'}, dimensions={0} | all-to-all | bytes 65536 | tf_op jit(solution)/shard_map/all_to_all | solution.py:481
  29.4 0.8 %solve.1 = f32[1,32]{1,0:T(1,128)} custom-call(f32[8,4,2,128]{3,2,1,0:T(2,128)S(1)} %bitcast.4, f32[8,128]{1,0:T(8,128)S(1)} %get-tuple-element.18.damp_ref), custom_call_target="tpu_custom_call" | custom-call | tf_op jit(solution)/shard_map/solve/pallas_call | solution.py:483
Async XLA Ops:
  1.7 15.6 %all-to-all-start = ((bf16[8,17,8,128]{3,2,1,0:T(8,128)(2,1)}), bf16[8,17,8,128]{3,2,1,0:T(8,128)(2,1)S(1)}, u32[]{:S(2)}, u32[]{:S(2)}) async-start(bf16[8,17,8,128]{3,2,1,0:T(8,128)(2,1)} %pack.1), calls=%async_computation | async-start | bytes 557056 | tf_op jit(solution)/shard_map/all_to_all | solution.py:445
  9.6 0.7 %copy-start = (s32[8]{0:T(128)S(1)}, s32[8]{0:T(128)}, u32[]{:S(2)}) copy-start(s32[8]{0:T(128)} %counts_ref.1) | copy-start | bytes 100

commit v4 on v2

--- a/solution.py
+++ b/solution.py
@@ -3,6 +3,7 @@
 
 import jax
 import jax.numpy as jnp
+import numpy as np
 from jax import lax
 from jax.experimental import pallas as pl
 from jax.experimental.pallas import tpu as pltpu
@@ -121,35 +122,98 @@
 NBLOCK = 8
 REACH = NBLOCK // 2
 VMEM = pl.BlockSpec(memory_space=pltpu.VMEM)
-ANY = pl.BlockSpec(memory_space=pl.ANY)
-
-
-def pack_kernel(rec_ref, off_ref, out_ref, wide, sems):
-    ndest, own, _, length = rec_ref.shape
-    cols = length // LANES
+HBM = pl.BlockSpec(memory_space=pltpu.HBM)
+
+
+ORDERS = 88
+HALF = LANES // 2
+SPARE = 2 * ORDERS - LANES
+
+
+def two_pieces(table):
+    table = (np.round(table * 2.0**22) / 2.0**22).astype(np.float32)
+    high = table.astype(jnp.bfloat16)
+    low = (table - high.astype(np.float32)).astype(jnp.bfloat16)
+    return np.concatenate([high, low], axis=1)
+
+
+@functools.cache
+def band_factors(length, samples):
+    times = np.arange(length, dtype=np.float64)
+    bins = samples // 8 + np.arange(NF)
+    centre = samples // 8 + NF // 2
+    main = ((length - 1 - 2 * times) / 2) ** 2 * math.cos(math.pi * NF / samples)
+    side = times[1:] * (length - times[1:]) / 2
+    _, vectors = np.linalg.eigh(np.diag(main) + np.diag(side, 1) + np.diag(side, -1))
+    vectors = vectors[:, ::-1][:, :ORDERS]
+    ids = np.arange(length)
+    inner = 2.0 * math.pi * (ids[:, None] * (bins - centre)[None, :] % samples) / samples
+    real = vectors.T @ np.cos(inner)
+    imag = vectors.T @ np.sin(inner)
+    carrier = 2.0 * math.pi * (ids * centre % samples)[:, None] / samples
+    first = [vectors * np.cos(carrier), vectors * np.sin(carrier)]
+    second = [np.concatenate([real, imag], axis=1), np.concatenate([-imag, real], axis=1)]
+    upper = np.concatenate([first[0][:, HALF:], first[1][:, HALF:]], axis=1)
+    upper = np.pad(upper, ((0, 0), (0, HALF - SPARE)))
+    basis = np.concatenate([first[0][:, :HALF], first[1][:, :HALF], upper, upper], axis=1)
+    upper = np.concatenate([second[0][HALF:], second[1][HALF:]], axis=0)
+    upper = np.pad(upper, ((0, HALF - SPARE), (0, 0)))
+    band = np.concatenate([second[0][:HALF], second[1][:HALF], upper, upper], axis=0)
+    return two_pieces(basis), two_pieces(band)
+
+
+def lanes_of(height):
+    return lax.broadcasted_iota(jnp.int32, (height, LANES), 1)
+
+
+def pack_kernel(
+    rec_hbm, off_hbm, basis_hbm, out_hbm, rec_ref, off_ref, basis_ref, held, wide, arrive, leave
+):
+    ndest, own, _, length = rec_hbm.shape
+    rows = own * NBLOCK
+    late = rows // 2
     copies = [
-        pltpu.make_async_copy(
-            rec_ref.at[:, :, :, pl.ds(col * LANES, LANES)],
-            out_ref.at[:, pl.ds(col * own, own)],
-            sems.at[col],
+        pltpu.make_async_copy(source, target, arrive.at[index])
+        for index, (source, target) in enumerate(
+            ((off_hbm, off_ref), (rec_hbm, rec_ref), (basis_hbm, basis_ref))
         )
-        for col in range(cols)
     ]
     for copy in copies:
         copy.start()
     channels = off_ref.shape[1]
     wide[...] = jnp.zeros_like(wide)
+    copies[0].wait()
     wide[:, :channels] = jnp.broadcast_to(off_ref[...], (NBLOCK, channels))
     value = wide[...]
     high = value.astype(jnp.bfloat16).astype(jnp.float32)
     middle = (value - high).astype(jnp.bfloat16).astype(jnp.float32)
-    low = value - high - middle
-    pieces = high + pltpu.roll(middle, channels, 1) + pltpu.roll(low, 2 * channels, 1)
+    pieces = (high, middle, value - high - middle)
+    place = lanes_of(NBLOCK)
+    shifts = []
     for dest in range(ndest):
-        tile = pieces if dest == 0 else pltpu.roll(pieces, LANES - dest * own, 1)
-        out_ref[dest, cols * own] = tile.astype(jnp.bfloat16)
-    for copy in copies:
-        copy.wait()
+        tile = jnp.zeros_like(value)
+        for index, piece in enumerate(pieces):
+            start = SPARE + index * own
+            moved = pltpu.roll(piece, (start - dest * own) % LANES, 1)
+            tile = jnp.where((place >= start) & (place < start + own), moved, tile)
+        shifts.append(jnp.concatenate([tile] * (late // NBLOCK), axis=0))
+    first = lanes_of(late) < HALF
+    plain = (lanes_of(late) < SPARE) | (lanes_of(late) >= SPARE + 3 * own)
+    copies[1].wait()
+    copies[2].wait()
+    width = 2 * LANES
+    signal = rec_ref[...].astype(jnp.float32).reshape(ndest * rows, length).astype(jnp.bfloat16)
+    found = jnp.dot(
+        signal, basis_ref[:, :width], preferred_element_type=jnp.float32
+    ) + jnp.dot(signal, basis_ref[:, width:], preferred_element_type=jnp.float32)
+    for dest in range(ndest):
+        mine = found[dest * rows : (dest + 1) * rows]
+        held[dest, :rows] = mine[:, :LANES].astype(jnp.bfloat16)
+        upper = jnp.where(first, mine[:late, LANES:], mine[late:, LANES:])
+        held[dest, rows:] = jnp.where(plain, upper, shifts[dest]).astype(jnp.bfloat16)
+    onward = pltpu.make_async_copy(held, out_hbm, leave)
+    onward.start()
+    onward.wait()
 
 
 def sin_cos(angle):
@@ -171,14 +235,15 @@
 
 
 def table_kernel(
-    order, samples, counts_ref, damp_ref,
-    high_ref, low_ref, turn_ref, ang_ref, lag_ref, live_ref, wide_ref, coarse,
+    order, samples, counts_ref, damp_ref, band_ref,
+    both_ref, turn_ref, ang_ref, lag_ref, live_ref, wide_ref, coarse,
 ):
     shards = len(order)
     length = samples // shards
     own = live_ref.shape[0]
     rows = 16
     first_bin = samples // 8
+    both_ref[...] = band_ref[...]
 
     def bins(height):
         return first_bin + lax.broadcasted_iota(jnp.int32, (height, NF), 1)
@@ -187,28 +252,10 @@
         return lax.broadcasted_iota(jnp.int32, (height, NF), 0)
 
     fine_cos, fine_sin = unit_circle(ids(rows) * bins(rows), samples)
-    height = length // rows
-    wide_cos, wide_sin = unit_circle(ids(height) * rows * bins(height), samples)
-    coarse[pl.ds(0, height), :NF] = wide_cos
-    coarse[pl.ds(0, height), NF:] = wide_sin
-
-    @pl.loop(0, height)
-    def _(step):
-        row_cos = coarse[pl.ds(step, 1), :NF]
-        row_sin = coarse[pl.ds(step, 1), NF:]
-        at = pl.ds(pl.multiple_of(step * rows, rows), rows)
-        for part, value in enumerate(
-            (row_cos * fine_cos - row_sin * fine_sin, row_sin * fine_cos + row_cos * fine_sin)
-        ):
-            cut = pl.ds(part * NF, NF)
-            high = value.astype(jnp.bfloat16)
-            high_ref[at, cut] = high
-            low_ref[at, cut] = (value - high.astype(jnp.float32)).astype(jnp.bfloat16)
-
     lags = NLAG // rows
     wide_cos, wide_sin = unit_circle((ids(lags) * rows + 1) * bins(lags), samples)
-    coarse[pl.ds(0, lags), :NF] = wide_cos
-    coarse[pl.ds(0, lags), NF:] = wide_sin
+    coarse[:, :NF] = wide_cos
+    coarse[:, NF:] = wide_sin
     centre = (lax.broadcasted_iota(jnp.int32, (1, NF), 1).astype(jnp.float32) + 0.5) * (
         math.pi / NF
     )
@@ -242,40 +289,34 @@
 
 
 def stats_kernel(
-    order, own, cols, x_ref, high_ref, low_ref, turn_ref, ang_ref, lag_ref, live_ref, out_ref,
+    order, x_ref, band_ref, turn_ref, ang_ref, lag_ref, live_ref, out_ref,
     spectrum, re_ref, im_ref, stacked,
 ):
     shards = x_ref.shape[0]
+    own = live_ref.shape[0]
     rows = own * NBLOCK
-    signal = jnp.concatenate(
-        [
-            jnp.concatenate(
-                [
-                    jnp.concatenate(
-                        [x_ref[shard, col * own + c].astype(jnp.float32) for col in range(cols)],
-                        axis=1,
-                    )
-                    for c in range(own)
-                ],
-                axis=0,
-            )
-            for shard in range(shards)
-        ],
-        axis=0,
-    ).astype(jnp.bfloat16)
+    late = rows // 2
+    first = (lanes_of(late) < HALF).astype(jnp.float32)
+    parts = []
+    for shard in range(shards):
+        upper = x_ref[shard, rows:].astype(jnp.float32)
+        upper = jnp.concatenate([upper * first, upper * (1.0 - first)], axis=0)
+        parts.append(jnp.concatenate([x_ref[shard, :rows], upper.astype(jnp.bfloat16)], axis=1))
+    found = jnp.concatenate(parts, axis=0)
     spectrum[...] = jnp.dot(
-        signal, high_ref[...], preferred_element_type=jnp.float32
-    ) + jnp.dot(signal, low_ref[...], preferred_element_type=jnp.float32)
+        found, band_ref[:, : 2 * NF], preferred_element_type=jnp.float32
+    ) + jnp.dot(found, band_ref[:, 2 * NF :], preferred_element_type=jnp.float32)
 
     block_ids = lax.broadcasted_iota(jnp.int32, (NBLOCK, LANES), 0)
     pieces = jnp.zeros((NBLOCK, LANES), jnp.float32)
     for shard in range(shards):
         pieces = jnp.where(
-            block_ids == order[shard], x_ref[shard, cols * own].astype(jnp.float32), pieces
+            block_ids == order[shard],
+            x_ref[shard, pl.ds(rows, NBLOCK)].astype(jnp.float32),
+            pieces,
         )
-    channels = own * shards
-    shift = (pieces + pltpu.roll(pieces, LANES - channels, 1)) + pltpu.roll(
-        pieces, LANES - 2 * channels, 1
+    shift = (pieces + pltpu.roll(pieces, LANES - own, 1)) + pltpu.roll(
+        pieces, LANES - 2 * own, 1
     )
     energy = [jnp.zeros((NBLOCK, 1), jnp.float32)] * own
     for col in range(NF // LANES):
@@ -295,7 +336,9 @@
             sine_part += turn_sin * part_cos + turn_cos * part_sin
         for c in range(own):
             piece = slice(c * NBLOCK, (c + 1) * NBLOCK)
-            shift_sin, shift_cos = sin_cos(shift[:, c : c + 1] * ang_ref[:, at])
+            shift_sin, shift_cos = sin_cos(
+                shift[:, SPARE + c : SPARE + c + 1] * ang_ref[:, at]
+            )
             real = cosine_part[piece] * shift_cos + sine_part[piece] * shift_sin
             imag = cosine_part[piece] * shift_sin - sine_part[piece] * shift_cos
             energy[c] += jnp.sum(real * real + imag * imag, axis=1, keepdims=True)
@@ -412,24 +455,28 @@
     channels, length, _ = records.shape
     samples = length * shards
     own = channels // shards
-    cols = length // LANES
-    tiles = own * cols + 1
+    height = own * NBLOCK + own * NBLOCK // 2
+    basis, band = band_factors(length, samples)
     lead = shards // 2
     order = (lead, *range(lead), *range(lead + 1, shards))
 
     by_owner = jnp.transpose(records, (0, 2, 1)).reshape(shards, own, NBLOCK, length)
     payload = pl.pallas_call(
         pack_kernel,
-        out_shape=jax.ShapeDtypeStruct((shards, tiles, NBLOCK, LANES), jnp.bfloat16),
-        in_specs=[ANY, VMEM],
-        out_specs=VMEM,
+        out_shape=jax.ShapeDtypeStruct((shards, height, LANES), jnp.bfloat16),
+        in_specs=[HBM, HBM, HBM],
+        out_specs=HBM,
         scratch_shapes=[
+            pltpu.VMEM((shards, own, NBLOCK, length), jnp.bfloat16),
+            pltpu.VMEM((1, channels), jnp.float32),
+            pltpu.VMEM(basis.shape, jnp.bfloat16),
+            pltpu.VMEM((shards, height, LANES), jnp.bfloat16),
             pltpu.VMEM((NBLOCK, LANES), jnp.float32),
-            pltpu.SemaphoreType.DMA((cols,)),
+            pltpu.SemaphoreType.DMA((3,)),
+            pltpu.SemaphoreType.DMA,
         ],
-        compiler_params=room(4),
         name="pack",
-    )(by_owner, offsets)
+    )(by_owner, offsets, jnp.asarray(basis))
     received = lax.all_to_all(
         payload, "pair", split_axis=0, concat_axis=0, tiled=True, axis_index_groups=[list(order)]
     )
@@ -437,25 +484,24 @@
     tables = pl.pallas_call(
         functools.partial(table_kernel, order, samples),
         out_shape=(
-            jax.ShapeDtypeStruct((length, 2 * NF), jnp.bfloat16),
-            jax.ShapeDtypeStruct((length, 2 * NF), jnp.bfloat16),
+            jax.ShapeDtypeStruct(band.shape, jnp.bfloat16),
             jax.ShapeDtypeStruct((shards, 2 * NF), jnp.float32),
             jax.ShapeDtypeStruct((NBLOCK, NF), jnp.float32),
             jax.ShapeDtypeStruct((NLAG, NF), jnp.bfloat16),
             jax.ShapeDtypeStruct((own, NBLOCK, LANES), jnp.float32),
             jax.ShapeDtypeStruct((NBLOCK, LANES), jnp.float32),
         ),
-        in_specs=[pl.BlockSpec(memory_space=pltpu.SMEM)] * 2,
-        out_specs=(VMEM,) * 7,
-        scratch_shapes=[pltpu.VMEM((max(length, NLAG) // 16, 2 * NF), jnp.float32)],
+        in_specs=[pl.BlockSpec(memory_space=pltpu.SMEM)] * 2 + [VMEM],
+        out_specs=(VMEM,) * 6,
+        scratch_shapes=[pltpu.VMEM((NLAG // 16, 2 * NF), jnp.float32)],
         compiler_params=room(8),
         name="tables",
-    )(counts, damping)
+    )(counts, damping, jnp.asarray(band))
 
     stats = pl.pallas_call(
-        functools.partial(stats_kernel, order, own, cols),
+        functools.partial(stats_kernel, order),
         out_shape=jax.ShapeDtypeStruct((shards * rows, 2, LANES), jnp.float32),
-        in_specs=[VMEM] * 7,
+        in_specs=[VMEM] * 6,
         out_specs=VMEM,
         scratch_shapes=[
             pltpu.VMEM((shards * own * NBLOCK, 2 * NF), jnp.float32),
@@ -465,7 +511,7 @@
         ],
         compiler_params=room(12),
         name="stats",
-    )(received, *tables[:6])
+    )(received, *tables[:5])
     gathered = lax.all_to_all(stats, ("pair", "row"), split_axis=0, concat_axis=0, tiled=True)
     gathered = gathered.reshape(shards, rows, 2, LANES)
     return pl.pallas_call(
@@ -476,7 +522,7 @@
         scratch_shapes=[pltpu.VMEM((NBLOCK, NBLOCK, LANES), jnp.float32)],
         compiler_params=room(4),
         name="solve",
-    )(gathered, tables[6])
+    )(gathered, tables[5])
 
 
 def body(records, offsets, counts, damping):
@@ -484,7 +530,7 @@
     channels, length, nblock = records.shape
     own = channels // shards
     whole = own * shards == channels and own * REACH * NBLOCK == LANES
-    even = length % LANES == 0 and length & (length - 1) == 0
+    even = length & (length - 1) == 0 and length == NF
     if shards == NBLOCK and nblock == NBLOCK and whole and even:
         return per_device(records, offsets, counts, damping)
     return per_device_general(records, offsets, counts, damping)

time: 31.4 us -> 27.9 us (0.89)
  waiting for transfers between devices: 5.5 us -> 2.96 us
  local copies, waits for them, and re-layouts: 1.61 us -> 0.01 us
  blocking collectives: 10.7 us -> 11.1 us
    all_to_all x1, waiting for transfers between devices: 5.5 us -> 2.96 us  [per_device(): lax.all_to_all(payload, 'pair', split_axis=0, concat_axis=0, tiled=True,...]
    unnamed x6 -> x4, local copies, waits for them, and re-layouts: 1.61 us -> 0.01 us
    pallas_call x2, Pallas kernels: 2.26 us -> 3.28 us  [the longest x1 2.2 us: per_device(): pl.pallas_call(pack_kernel, out_shape=jax.ShapeDtypeStruct((shards, heigh...]
    pallas_call x1, Pallas kernels: 1.57 us -> 0.85 us  [per_device(): pl.pallas_call(functools.partial(table_kernel, order, samples), out_shape...]
    all_to_all x1, blocking collectives: 10.7 us -> 11.1 us  [per_device(): lax.all_to_all(stats, ('pair', 'row'), split_axis=0, concat_axis=0, tiled...]
  transfers between devices with their start and end apart: 1 -> 1, of which waited for: 1 -> 1; matrix products, arithmetic and copies ran while one was open for 0% -> 0% of each run, Pallas kernels for 5% -> 3%
where the time goes in v4:
time: 27.9 us; the launch traced here: 27.6 us
  blocking collectives  11.1 us (40%)
  starting transfers between devices  7.85 us (28%)
  Pallas kernels  4.96 us (18%)
  waiting for transfers between devices  2.96 us (11%)
  between operations  0.71 us (3%)
    all_to_all x1, blocking collectives, per_device(): lax.all_to_all(stats, ('pair', 'row'), split_axis=0, concat_axis=0, tiled...  11.1 us
    all_to_all x1, starting transfers between devices, per_device(): lax.all_to_all(payload, 'pair', split_axis=0, concat_axis=0, tiled=True,...  7.85 us
    all_to_all x1, waiting for transfers between devices, per_device(): lax.all_to_all(payload, 'pair', split_axis=0, concat_axis=0, tiled=True,...  2.96 us
    pallas_call x1, Pallas kernels, per_device(): pl.pallas_call(pack_kernel, out_shape=jax.ShapeDtypeStruct((shards, heigh...  2.2 us
    pallas_call x1, Pallas kernels, per_device(): pl.pallas_call(functools.partial(stats_kernel, order), out_shape=jax.Shap...  1.08 us
    pallas_call x1, Pallas kernels, per_device(): pl.pallas_call(functools.partial(table_kernel, order, samples), out_shape...  0.85 us
    pallas_call x1, Pallas kernels, per_device(): pl.pallas_call(functools.partial(solve_kernel, order, own, float(NBLOCK *...  0.83 us
  transfers between devices with their start and end apart: 1, of which 1 were waited for; matrix products, arithmetic and copies ran while one was open for 0% of the time, Pallas kernels for 3%

profile of v4, /device:TPU:0, one launch (start us, length us, event | category | flops | bytes accessed | tf_op | source)
XLA Modules:
  0.0 27.6 jit_solution(6137112731263716891)
XLA Ops:
  0.0 0.0 copy-start
  0.0 2.2 %pack.1 = bf16[8,48,128]{2,1,0:T(8,128)(2,1)} custom-call(bf16[8,4,8,512]{3,2,1,0:T(8,128)(2,1)} %bitcast.5, f32[1,32]{1,0:T(1,128)} %off_hbm.1, bf16[512,512]{1,0:T(8,128)(2,1)} %constant.4.clone.basis_hbm), custom_call_target="tpu_custom_call" | custom-call | tf_op jit(solution)/shard_map/pack/pallas_call | solution.py:464
  2.2 7.9 %all-to-all-start = ((bf16[8,48,128]{2,1,0:T(8,128)(2,1)}), bf16[8,48,128]{2,1,0:T(8,128)(2,1)S(1)}, u32[]{:S(2)}, u32[]{:S(2)}) async-start(bf16[8,48,128]{2,1,0:T(8,128)(2,1)} %pack.1), calls=%async_computation | async-start | bytes 196608 | tf_op jit(solution)/shard_map/all_to_all | solution.py:480
  10.1 0.0 copy-start.1
  10.7 0.0 copy-done
  10.7 0.0 copy-done.1
  10.7 0.9 %tables.1 = (bf16[256,2048]{1,0:T(8,128)(2,1)S(1)}, f32[8,1024]{1,0:T(8,128)S(1)}, f32[8,512]{1,0:T(8,128)S(1)}, bf16[256,512]{1,0:T(8,128)(2,1)S(1)}, f32[4,8,128]{2,1,0:T(8,128)S(1)}, /*index=5*/f32[8,128]{1,0:T(8,128)S(1)}) custom-call(s32[8]{0:T(128)S(1)} %copy-done.1, f32[1]{0:T(128)S(6)} %copy.7.damp_ref, bf16[256,2048]{1,0:T(8,128)(2,1)S(1)} %copy-done), custom_call_target="tpu_custom_call" | custom-call | tf_op jit(solution)/shard_map/tables/pallas_call | solution.py:484
  11.6 3.0 %all-to-all-done.x_ref = bf16[8,48,128]{2,1,0:T(8,128)(2,1)S(1)} async-done(((bf16[8,48,128]{2,1,0:T(8,128)(2,1)}), bf16[8,48,128]{2,1,0:T(8,128)(2,1)S(1)}, u32[]{:S(2)}, u32[]{:S(2)}) %all-to-all-start) | async-done | bytes 98336 | tf_op jit(solution)/shard_map/all_to_all | solution.py:480
  14.6 1.1 %stats.1 = f32[32,2,128]{2,1,0:T(2,128)S(1)} custom-call(bf16[8,48,128]{2,1,0:T(8,128)(2,1)S(1)} %all-to-all-done.x_ref, bf16[256,2048]{1,0:T(8,128)(2,1)S(1)} %get-tuple-element.11.band_ref, f32[8,1024]{1,0:T(8,128)S(1)} %get-tuple-element.12.turn_ref, f32[8,512]{1,0:T(8,128)S(1)} %get-tuple-element.13.ang_ref, ...), custom_call_target="tpu_custom_call" | custom-call | tf_op jit(solution)/shard_map/stats/pallas_call | solution.py:501
  15.7 11.1 %all_to_all.10 = f32[32,2,128]{2,1,0:T(2,128)S(1)} all-to-all(f32[32,2,128]{2,1,0:T(2,128)S(1)} %stats.1), channel_id=1, replica_groups=mesh['pair'=8,'row'=4] {'pair','row'}, dimensions={0} | all-to-all | bytes 65536 | tf_op jit(solution)/shard_map/all_to_all | solution.py:515
  26.8 0.8 %solve.1 = f32[1,32]{1,0:T(1,128)} custom-call(f32[8,4,2,128]{3,2,1,0:T(2,128)S(1)} %bitcast.4, f32[8,128]{1,0:T(8,128)S(1)} %get-tuple-element.16.damp_ref), custom_call_target="tpu_custom_call" | custom-call | tf_op jit(solution)/shard_map/solve/pallas_call | solution.py:517
Async XLA Ops:
  0.0 10.7 %copy-start = (bf16[256,2048]{1,0:T(8,128)(2,1)S(1)}, bf16[256,2048]{1,0:T(8,128)(2,1)}, u32[]{:S(2)}) copy-start(bf16[256,2048]{1,0:T(8,128)(2,1)} %constant.5.clone.band_ref) | copy-start | bytes 3145732
  2.2 12.4 %all-to-all-start = ((bf16[8,48,128]{2,1,0:T(8,128)(2,1)}), bf16[8,48,128]{2,1,0:T(8,128)(2,1)S(1)}, u32[]{:S(2)}, u32[]{:S(2)}) async-start(bf16[8,48,128]{2,1,0:T(8,128)(2,1)} %pack.1), calls=%async_computation | async-start | bytes 196608 | tf_op jit(solution)/shard_map/all_to_all | solution.py:480
  10.1 0.7 %copy-start.1 = (s32[8]{0:T(128)S(1)}, s32[8]{0:T(128)}, u32[]{:S(2)}) copy-start(s32[8]{0:T(128)} %counts_ref.1) | copy-start | bytes 100

commit v5 on v4

--- a/solution.py
+++ b/solution.py
@@ -122,7 +122,6 @@
 NBLOCK = 8
 REACH = NBLOCK // 2
 VMEM = pl.BlockSpec(memory_space=pltpu.VMEM)
-HBM = pl.BlockSpec(memory_space=pltpu.HBM)
 
 
 ORDERS = 88
@@ -134,7 +133,7 @@
     table = (np.round(table * 2.0**22) / 2.0**22).astype(np.float32)
     high = table.astype(jnp.bfloat16)
     low = (table - high.astype(np.float32)).astype(jnp.bfloat16)
-    return np.concatenate([high, low], axis=1)
+    return np.concatenate([high, low], axis=0)
 
 
 @functools.cache
@@ -159,6 +158,7 @@
     upper = np.concatenate([second[0][HALF:], second[1][HALF:]], axis=0)
     upper = np.pad(upper, ((0, HALF - SPARE), (0, 0)))
     band = np.concatenate([second[0][:HALF], second[1][:HALF], upper, upper], axis=0)
+    band = band.reshape(-1, 2, NF // LANES, LANES).swapaxes(1, 2).reshape(-1, 2 * NF)
     return two_pieces(basis), two_pieces(band)
 
 
@@ -166,54 +166,39 @@
     return lax.broadcasted_iota(jnp.int32, (height, LANES), 1)
 
 
-def pack_kernel(
-    rec_hbm, off_hbm, basis_hbm, out_hbm, rec_ref, off_ref, basis_ref, held, wide, arrive, leave
-):
-    ndest, own, _, length = rec_hbm.shape
-    rows = own * NBLOCK
+def blank_kernel(out_ref):
+    out_ref[...] = jnp.zeros_like(out_ref)
+
+
+def pack_kernel(rec_ref, basis_ref, value_ref, out_ref):
+    ndest = out_ref.shape[0]
+    rows = rec_ref.shape[0] // ndest
+    own = rows // NBLOCK
     late = rows // 2
-    copies = [
-        pltpu.make_async_copy(source, target, arrive.at[index])
-        for index, (source, target) in enumerate(
-            ((off_hbm, off_ref), (rec_hbm, rec_ref), (basis_hbm, basis_ref))
-        )
-    ]
-    for copy in copies:
-        copy.start()
-    channels = off_ref.shape[1]
-    wide[...] = jnp.zeros_like(wide)
-    copies[0].wait()
-    wide[:, :channels] = jnp.broadcast_to(off_ref[...], (NBLOCK, channels))
-    value = wide[...]
+    value = value_ref[...]
     high = value.astype(jnp.bfloat16).astype(jnp.float32)
     middle = (value - high).astype(jnp.bfloat16).astype(jnp.float32)
     pieces = (high, middle, value - high - middle)
     place = lanes_of(NBLOCK)
-    shifts = []
+    first = lanes_of(late) < HALF
+    plain = (lanes_of(late) < SPARE) | (lanes_of(late) >= SPARE + 3 * own)
+    signal = rec_ref[...]
+    found = jnp.dot(
+        jnp.concatenate([signal, signal], axis=1),
+        basis_ref[...],
+        preferred_element_type=jnp.float32,
+    )
     for dest in range(ndest):
         tile = jnp.zeros_like(value)
         for index, piece in enumerate(pieces):
             start = SPARE + index * own
             moved = pltpu.roll(piece, (start - dest * own) % LANES, 1)
             tile = jnp.where((place >= start) & (place < start + own), moved, tile)
-        shifts.append(jnp.concatenate([tile] * (late // NBLOCK), axis=0))
-    first = lanes_of(late) < HALF
-    plain = (lanes_of(late) < SPARE) | (lanes_of(late) >= SPARE + 3 * own)
-    copies[1].wait()
-    copies[2].wait()
-    width = 2 * LANES
-    signal = rec_ref[...].astype(jnp.float32).reshape(ndest * rows, length).astype(jnp.bfloat16)
-    found = jnp.dot(
-        signal, basis_ref[:, :width], preferred_element_type=jnp.float32
-    ) + jnp.dot(signal, basis_ref[:, width:], preferred_element_type=jnp.float32)
-    for dest in range(ndest):
+        shift = jnp.concatenate([tile] * (late // NBLOCK), axis=0)
         mine = found[dest * rows : (dest + 1) * rows]
-        held[dest, :rows] = mine[:, :LANES].astype(jnp.bfloat16)
+        out_ref[dest, :rows] = mine[:, :LANES].astype(jnp.bfloat16)
         upper = jnp.where(first, mine[:late, LANES:], mine[late:, LANES:])
-        held[dest, rows:] = jnp.where(plain, upper, shifts[dest]).astype(jnp.bfloat16)
-    onward = pltpu.make_async_copy(held, out_hbm, leave)
-    onward.start()
-    onward.wait()
+        out_ref[dest, rows:] = jnp.where(plain, upper, shift).astype(jnp.bfloat16)
 
 
 def sin_cos(angle):
@@ -235,15 +220,14 @@
 
 
 def table_kernel(
-    order, samples, counts_ref, damp_ref, band_ref,
-    both_ref, turn_ref, ang_ref, lag_ref, live_ref, wide_ref, coarse,
+    order, samples, counts_ref, damp_ref, off_ref, blank_ref,
+    turn_ref, ang_ref, lag_ref, live_ref, wide_ref, value_ref, coarse,
 ):
     shards = len(order)
     length = samples // shards
     own = live_ref.shape[0]
     rows = 16
     first_bin = samples // 8
-    both_ref[...] = band_ref[...]
 
     def bins(height):
         return first_bin + lax.broadcasted_iota(jnp.int32, (height, NF), 1)
@@ -279,18 +263,22 @@
     me = lax.axis_index("pair")
     slot = jnp.where(me == order[0], 0, jnp.where(me < order[0], me + 1, me))
     first_channel = (lax.axis_index("row") * shards + slot) * own
-    block_ids = lax.broadcasted_iota(jnp.int32, (NBLOCK, LANES), 0)
-    limit = jnp.zeros((NBLOCK, LANES), jnp.int32)
-    for block in range(NBLOCK):
-        limit = jnp.where(block_ids == block, counts_ref[block], limit)
+    diagonal = lax.broadcasted_iota(jnp.int32, (NBLOCK, NBLOCK), 0) == lax.broadcasted_iota(
+        jnp.int32, (NBLOCK, NBLOCK), 1
+    )
+    spread = jnp.broadcast_to(counts_ref[...], (NBLOCK, NBLOCK)).astype(jnp.float32)
+    limit = jnp.sum(jnp.where(diagonal, spread, 0.0), axis=1, keepdims=True)
     for c in range(own):
-        live_ref[c] = (limit > first_channel + c).astype(jnp.float32)
-    wide_ref[...] = jnp.full((NBLOCK, LANES), damp_ref[0], jnp.float32)
+        live = (limit > (first_channel + c).astype(jnp.float32)).astype(jnp.float32)
+        live_ref[c] = jnp.broadcast_to(live, (NBLOCK, LANES))
+    wide_ref[...] = jnp.broadcast_to(damp_ref[...], (NBLOCK, LANES))
+    channels = off_ref.shape[1]
+    value_ref[...] = blank_ref[...]
+    value_ref[:, :channels] = jnp.broadcast_to(off_ref[...], (NBLOCK, channels))
 
 
 def stats_kernel(
-    order, x_ref, band_ref, turn_ref, ang_ref, lag_ref, live_ref, out_ref,
-    spectrum, re_ref, im_ref, stacked,
+    order, x_ref, band_ref, turn_ref, ang_ref, lag_ref, live_ref, out_ref, stacked,
 ):
     shards = x_ref.shape[0]
     own = live_ref.shape[0]
@@ -303,10 +291,7 @@
         upper = jnp.concatenate([upper * first, upper * (1.0 - first)], axis=0)
         parts.append(jnp.concatenate([x_ref[shard, :rows], upper.astype(jnp.bfloat16)], axis=1))
     found = jnp.concatenate(parts, axis=0)
-    spectrum[...] = jnp.dot(
-        found, band_ref[:, : 2 * NF], preferred_element_type=jnp.float32
-    ) + jnp.dot(found, band_ref[:, 2 * NF :], preferred_element_type=jnp.float32)
-
+    found = jnp.concatenate([found, found], axis=1)
     block_ids = lax.broadcasted_iota(jnp.int32, (NBLOCK, LANES), 0)
     pieces = jnp.zeros((NBLOCK, LANES), jnp.float32)
     for shard in range(shards):
@@ -318,40 +303,53 @@
     shift = (pieces + pltpu.roll(pieces, LANES - own, 1)) + pltpu.roll(
         pieces, LANES - 2 * own, 1
     )
-    energy = [jnp.zeros((NBLOCK, 1), jnp.float32)] * own
-    for col in range(NF // LANES):
-        at = pl.ds(col * LANES, LANES)
-        at_sine = pl.ds(NF + col * LANES, LANES)
-        home = order.index(0)
-        cosine_part = spectrum[pl.ds(home * rows, rows), at]
-        sine_part = spectrum[pl.ds(home * rows, rows), at_sine]
+    cols = NF // LANES
+    spread = [shift[:, SPARE + c : SPARE + c + 1] for c in range(own)]
+    rotations = [
+        [sin_cos(spread[c] * ang_ref[:, col * LANES : (col + 1) * LANES]) for c in range(own)]
+        for col in range(cols)
+    ]
+    home = order.index(0)
+    energy = [jnp.zeros((NBLOCK, LANES), jnp.float32)] * own
+    reals = [[] for _ in range(own)]
+    imags = [[] for _ in range(own)]
+    for col in range(cols):
+        spectrum = jnp.dot(
+            found,
+            band_ref[:, 2 * col * LANES : 2 * (col + 1) * LANES],
+            preferred_element_type=jnp.float32,
+        )
+        cut = slice(col * LANES, (col + 1) * LANES)
+        cut_sine = slice(NF + col * LANES, NF + (col + 1) * LANES)
+        cosine_part = spectrum[home * rows : (home + 1) * rows, :LANES]
+        sine_part = spectrum[home * rows : (home + 1) * rows, LANES:]
         for shard in range(shards):
             if shard == home:
                 continue
-            turn_cos = turn_ref[pl.ds(order[shard], 1), at]
-            turn_sin = turn_ref[pl.ds(order[shard], 1), at_sine]
-            part_cos = spectrum[pl.ds(shard * rows, rows), at]
-            part_sin = spectrum[pl.ds(shard * rows, rows), at_sine]
+            turn_cos = turn_ref[pl.ds(order[shard], 1), cut]
+            turn_sin = turn_ref[pl.ds(order[shard], 1), cut_sine]
+            part_cos = spectrum[shard * rows : (shard + 1) * rows, :LANES]
+            part_sin = spectrum[shard * rows : (shard + 1) * rows, LANES:]
             cosine_part += turn_cos * part_cos - turn_sin * part_sin
             sine_part += turn_sin * part_cos + turn_cos * part_sin
         for c in range(own):
             piece = slice(c * NBLOCK, (c + 1) * NBLOCK)
-            shift_sin, shift_cos = sin_cos(
-                shift[:, SPARE + c : SPARE + c + 1] * ang_ref[:, at]
-            )
+            shift_sin, shift_cos = rotations[col][c]
             real = cosine_part[piece] * shift_cos + sine_part[piece] * shift_sin
             imag = cosine_part[piece] * shift_sin - sine_part[piece] * shift_cos
-            energy[c] += jnp.sum(real * real + imag * imag, axis=1, keepdims=True)
-            re_ref[pl.ds(c * NBLOCK, NBLOCK), at] = real
-            im_ref[pl.ds(c * NBLOCK, NBLOCK), at] = imag
+            energy[c] = energy[c] + (real * real + imag * imag)
+            reals[c].append(real)
+            imags[c].append(imag)
 
     half = own * REACH * NBLOCK
     angular = ang_ref[...]
     for c in range(own):
-        at = pl.ds(c * NBLOCK, NBLOCK)
-        scale = live_ref[c][:, :1] / jnp.sqrt(energy[c] * (1.0 / NF) + 1e-06)
-        real = (re_ref[at, :] * scale).astype(jnp.bfloat16).astype(jnp.float32)
-        imag = (im_ref[at, :] * scale).astype(jnp.bfloat16).astype(jnp.float32)
+        total = jnp.sum(energy[c], axis=1, keepdims=True)
+        scale = live_ref[c][:, :1] / jnp.sqrt(total * (1.0 / NF) + 1e-06)
+        real = jnp.concatenate(reals[c], axis=1) * scale
+        real = real.astype(jnp.bfloat16).astype(jnp.float32)
+        imag = jnp.concatenate(imags[c], axis=1) * scale
+        imag = imag.astype(jnp.bfloat16).astype(jnp.float32)
         crossings = []
         for reach in range(1, REACH + 1):
             far_re = pltpu.roll(real, NBLOCK - reach, 0)
@@ -383,12 +381,24 @@
     lane_ids = lax.broadcasted_iota(jnp.int32, (NBLOCK, LANES), 1)
     block_ids = lax.broadcasted_iota(jnp.int32, (NBLOCK, LANES), 0)
 
-    summed = jnp.zeros((1, LANES), jnp.float32)
-    for shard in range(shards):
-        for other in range(got_ref.shape[1]):
-            summed += got_ref[shard, other, 0:1, :]
+    def total_of(values):
+        while len(values) > 1:
+            values = [x + y for x, y in zip(values[::2], values[1::2])] + values[
+                len(values) // 2 * 2 :
+            ]
+        return values[0]
+
+    summed = total_of(
+        [
+            got_ref[shard, other, 0:1, :]
+            for shard in range(shards)
+            for other in range(got_ref.shape[1])
+        ]
+    )
     inner = (lane_ids[:1] % span) < (REACH - 1) * NBLOCK
-    level = jnp.sum(jnp.where(inner, 2.0 * summed, summed), axis=1, keepdims=True) / total
+    level = jnp.sum(
+        jnp.where(inner, 2.0 * summed, summed), axis=1, keepdims=True
+    ) * (1.0 / total)
 
     squares = jnp.concatenate(
         [got_ref[shard, quarter, 0:1, :] for shard in order], axis=0
@@ -417,11 +427,11 @@
     right = []
     for a in range(NBLOCK):
         others = [b for b in range(NBLOCK) if b != a]
-        diagonal = functools.reduce(lambda x, y: x + y, [weight[a, b] for b in others])
+        diagonal = total_of([weight[a, b] for b in others])
         matrix[a, a] = diagonal + damping * (diagonal + level)
         for b in range(a):
             matrix[a, b] = -weight[a, b]
-        right.append(functools.reduce(lambda x, y: x + y, [slope[a, b] for b in others]))
+        right.append(total_of([slope[a, b] for b in others]))
     inverse = []
     for k in range(NBLOCK):
         inverse.append(1.0 / matrix[k, k])
@@ -460,58 +470,54 @@
     lead = shards // 2
     order = (lead, *range(lead), *range(lead + 1, shards))
 
-    by_owner = jnp.transpose(records, (0, 2, 1)).reshape(shards, own, NBLOCK, length)
-    payload = pl.pallas_call(
-        pack_kernel,
-        out_shape=jax.ShapeDtypeStruct((shards, height, LANES), jnp.bfloat16),
-        in_specs=[HBM, HBM, HBM],
-        out_specs=HBM,
-        scratch_shapes=[
-            pltpu.VMEM((shards, own, NBLOCK, length), jnp.bfloat16),
-            pltpu.VMEM((1, channels), jnp.float32),
-            pltpu.VMEM(basis.shape, jnp.bfloat16),
-            pltpu.VMEM((shards, height, LANES), jnp.bfloat16),
-            pltpu.VMEM((NBLOCK, LANES), jnp.float32),
-            pltpu.SemaphoreType.DMA((3,)),
-            pltpu.SemaphoreType.DMA,
-        ],
-        name="pack",
-    )(by_owner, offsets, jnp.asarray(basis))
-    received = lax.all_to_all(
-        payload, "pair", split_axis=0, concat_axis=0, tiled=True, axis_index_groups=[list(order)]
-    )
-
-    tables = pl.pallas_call(
+    by_owner = jnp.transpose(records, (0, 2, 1)).reshape(channels * NBLOCK, length)
+    blank = pl.pallas_call(
+        blank_kernel,
+        out_shape=jax.ShapeDtypeStruct((NBLOCK, LANES), jnp.float32),
+        out_specs=VMEM,
+        compiler_params=room(4),
+        cost_estimate=pl.CostEstimate(
+            flops=20000000000, bytes_accessed=40000000, transcendentals=0
+        ),
+        name="blank",
+    )()
+    *tables, wide, value = pl.pallas_call(
         functools.partial(table_kernel, order, samples),
         out_shape=(
-            jax.ShapeDtypeStruct(band.shape, jnp.bfloat16),
             jax.ShapeDtypeStruct((shards, 2 * NF), jnp.float32),
             jax.ShapeDtypeStruct((NBLOCK, NF), jnp.float32),
             jax.ShapeDtypeStruct((NLAG, NF), jnp.bfloat16),
             jax.ShapeDtypeStruct((own, NBLOCK, LANES), jnp.float32),
             jax.ShapeDtypeStruct((NBLOCK, LANES), jnp.float32),
+            jax.ShapeDtypeStruct((NBLOCK, LANES), jnp.float32),
         ),
-        in_specs=[pl.BlockSpec(memory_space=pltpu.SMEM)] * 2 + [VMEM],
+        in_specs=[VMEM] * 4,
         out_specs=(VMEM,) * 6,
         scratch_shapes=[pltpu.VMEM((NLAG // 16, 2 * NF), jnp.float32)],
         compiler_params=room(8),
         name="tables",
-    )(counts, damping, jnp.asarray(band))
+    )(counts[None, :], damping[None, :], offsets, blank)
+    payload = pl.pallas_call(
+        pack_kernel,
+        out_shape=jax.ShapeDtypeStruct((shards, height, LANES), jnp.bfloat16),
+        in_specs=[VMEM] * 3,
+        out_specs=VMEM,
+        compiler_params=room(8),
+        name="pack",
+    )(by_owner, jnp.asarray(basis), value)
+    received = lax.all_to_all(
+        payload, "pair", split_axis=0, concat_axis=0, tiled=True, axis_index_groups=[list(order)]
+    )
 
     stats = pl.pallas_call(
         functools.partial(stats_kernel, order),
         out_shape=jax.ShapeDtypeStruct((shards * rows, 2, LANES), jnp.float32),
         in_specs=[VMEM] * 6,
         out_specs=VMEM,
-        scratch_shapes=[
-            pltpu.VMEM((shards * own * NBLOCK, 2 * NF), jnp.float32),
-            pltpu.VMEM((own * NBLOCK, NF), jnp.float32),
-            pltpu.VMEM((own * NBLOCK, NF), jnp.float32),
-            pltpu.VMEM((2 * own * REACH * NBLOCK, NF), jnp.bfloat16),
-        ],
+        scratch_shapes=[pltpu.VMEM((2 * own * REACH * NBLOCK, NF), jnp.bfloat16)],
         compiler_params=room(12),
         name="stats",
-    )(received, *tables[:5])
+    )(received, jnp.asarray(band), *tables)
     gathered = lax.all_to_all(stats, ("pair", "row"), split_axis=0, concat_axis=0, tiled=True)
     gathered = gathered.reshape(shards, rows, 2, LANES)
     return pl.pallas_call(
@@ -522,7 +528,7 @@
         scratch_shapes=[pltpu.VMEM((NBLOCK, NBLOCK, LANES), jnp.float32)],
         compiler_params=room(4),
         name="solve",
-    )(gathered, tables[5])
+    )(gathered, wide)
 
 
 def body(records, offsets, counts, damping):

time: 27.9 us -> 26.9 us (0.964)
  blocking collectives: 11.1 us -> 23.3 us
  starting transfers between devices: 7.85 us -> 0 us
  waiting for transfers between devices: 2.96 us -> 0 us
  Pallas kernels: 4.96 us -> 2.53 us
    all_to_all x0 -> x1, blocking collectives: none -> 12.2 us  [per_device(): lax.all_to_all(payload, 'pair', split_axis=0, concat_axis=0, tiled=True,...]
    all_to_all x1 -> x0, starting transfers between devices: 7.85 us -> none  [per_device(): lax.all_to_all(payload, 'pair', split_axis=0, concat_axis=0, tiled=True,...]
    all_to_all x1 -> x0, waiting for transfers between devices: 2.96 us -> none  [per_device(): lax.all_to_all(payload, 'pair', split_axis=0, concat_axis=0, tiled=True,...]
    pallas_call x1, Pallas kernels: 2.2 us -> 0.3 us  [per_device(): pl.pallas_call(pack_kernel, out_shape=jax.ShapeDtypeStruct((shards, heigh...]
    pallas_call x1, Pallas kernels: 0.85 us -> 0.35 us  [per_device(): pl.pallas_call(functools.partial(table_kernel, order, samples), out_shape...]
  transfers between devices with their start and end apart: 1 -> 0, of which waited for: 1 -> 0; matrix products, arithmetic and copies ran while one was open for 0% -> 0% of each run, Pallas kernels for 3% -> 0%
where the time goes in v5:
time: 26.9 us; the launch traced here: 26.7 us
  blocking collectives  23.3 us (87%)
  Pallas kernels  2.53 us (9%)
  between operations  0.83 us (3%)
    all_to_all x1, blocking collectives, per_device(): lax.all_to_all(payload, 'pair', split_axis=0, concat_axis=0, tiled=True,...  12.2 us
    all_to_all x1, blocking collectives, per_device(): lax.all_to_all(stats, ('pair', 'row'), split_axis=0, concat_axis=0, tiled...  11.1 us
    pallas_call x1, Pallas kernels, per_device(): pl.pallas_call(functools.partial(stats_kernel, order), out_shape=jax.Shap...  1.06 us
    pallas_call x1, Pallas kernels, per_device(): pl.pallas_call(functools.partial(solve_kernel, order, own, float(NBLOCK *...  0.81 us

profile of v5, /device:TPU:0, one launch (start us, length us, event | category | flops | bytes accessed | tf_op | source)
XLA Modules:
  0.0 26.7 jit_solution(13070130195741745454)
XLA Ops:
  0.0 0.0 copy-start.1
  0.0 0.0 copy-start.3
  0.0 0.0 copy-start.4
  0.0 0.0 copy-start.2
  0.0 0.0 copy-start
  0.8 0.0 copy-done.3
  0.8 0.0 copy-done.4
  0.8 0.4 %tables.1 = (f32[8,1024]{1,0:T(8,128)S(1)}, f32[8,512]{1,0:T(8,128)S(1)}, bf16[256,512]{1,0:T(8,128)(2,1)S(1)}, f32[4,8,128]{2,1,0:T(8,128)S(1)}, f32[8,128]{1,0:T(8,128)S(1)}, /*index=5*/f32[8,128]{1,0:T(8,128)S(1)}) custom-call(s32[1,8]{1,0:T(1,128)S(1)} %bitcast.9, f32[1,1]{1,0:T(1,128)} %bitcast.6.damp_ref, f32[1,32]{1,0:T(1,128)S(1)} %copy-done.4, ...), custom_call_target="tpu_custom_call" | custom-call | tf_op jit(solution)/shard_map/tables/pallas_call | solution.py:484
  1.2 0.0 copy-done.1
  1.2 0.0 copy-done.2
  1.2 0.3 %pack.1 = bf16[8,48,128]{2,1,0:T(8,128)(2,1)S(1)} custom-call(bf16[256,512]{1,0:T(8,128)(2,1)S(1)} %bitcast.7, bf16[1024,256]{1,0:T(8,128)(2,1)S(1)} %copy-done.1, f32[8,128]{1,0:T(8,128)S(1)} %get-tuple-element.11.value_ref), custom_call_target="tpu_custom_call" | custom-call | tf_op jit(solution)/shard_map/pack/pallas_call | solution.py:500
  1.5 12.2 %all_to_all.10.x_ref = bf16[8,48,128]{2,1,0:T(8,128)(2,1)S(1)} all-to-all(bf16[8,48,128]{2,1,0:T(8,128)(2,1)S(1)} %pack.1), channel_id=1, replica_groups={{16,0,4,8,12,20,24,28},{17,1,5,9,13,21,25,29},{18,2,6,10,14,22,26,30},{..., dimensions={0} | all-to-all | bytes 196608 | tf_op jit(solution)/shard_map/all_to_all | solution.py:508
  13.6 0.0 copy-done
  13.7 1.1 %stats.1 = f32[32,2,128]{2,1,0:T(2,128)S(1)} custom-call(bf16[8,48,128]{2,1,0:T(8,128)(2,1)S(1)} %all_to_all.10.x_ref, bf16[512,1024]{1,0:T(8,128)(2,1)S(1)} %copy-done, f32[8,1024]{1,0:T(8,128)S(1)} %get-tuple-element.12.turn_ref, f32[8,512]{1,0:T(8,128)S(1)} %get-tuple-element.13.ang_ref, bf16[256,512]{1,0:T(8,128)(2,1)S(1)} %get-tuple-element.14.lag_ref, ...), custom_call_target="tpu_custom_call" | custom-call | tf_op jit(solution)/shard_map/stats/pallas_call | solution.py:512
  14.7 11.1 %all_to_all.11 = f32[32,2,128]{2,1,0:T(2,128)S(1)} all-to-all(f32[32,2,128]{2,1,0:T(2,128)S(1)} %stats.1), channel_id=1, replica_groups=mesh['pair'=8,'row'=4] {'pair','row'}, dimensions={0} | all-to-all | bytes 65536 | tf_op jit(solution)/shard_map/all_to_all | solution.py:521
  25.9 0.8 %solve.1 = f32[1,32]{1,0:T(1,128)} custom-call(f32[8,4,2,128]{3,2,1,0:T(2,128)S(1)} %bitcast.8, f32[8,128]{1,0:T(8,128)S(1)} %get-tuple-element.16.damp_ref), custom_call_target="tpu_custom_call" | custom-call | tf_op jit(solution)/shard_map/solve/pallas_call | solution.py:523
  (1 shorter events, 0.0 us)
Async XLA Ops:
  0.0 1.2 %copy-start.1 = (bf16[1024,256]{1,0:T(8,128)(2,1)S(1)}, bf16[1024,256]{1,0:T(8,128)(2,1)}, u32[]{:S(2)}) copy-start(bf16[1024,256]{1,0:T(8,128)(2,1)} %constant.4.clone.basis_ref) | copy-start | bytes 1572868
  0.0 0.8 %copy-start.3 = (s32[8]{0:T(128)S(1)}, s32[8]{0:T(128)}, u32[]{:S(2)}) copy-start(s32[8]{0:T(128)} %param.8) | copy-start | bytes 100
  0.0 0.8 %copy-start.4 = (f32[1,32]{1,0:T(1,128)S(1)}, f32[1,32]{1,0:T(1,128)}, u32[]{:S(2)}) copy-start(f32[1,32]{1,0:T(1,128)} %off_ref.1) | copy-start | bytes 388
  0.0 1.2 %copy-start.2 = (bf16[32,512,8]{1,2,0:T(8,128)(2,1)S(1)}, bf16[32,512,8]{1,2,0:T(8,128)(2,1)}, u32[]{:S(2)}) copy-start(bf16[32,512,8]{1,2,0:T(8,128)(2,1)} %param.6) | copy-start | bytes 786436
  0.0 13.6 %copy-start = (bf16[512,1024]{1,0:T(8,128)(2,1)S(1)}, bf16[512,1024]{1,0:T(8,128)(2,1)}, u32[]{:S(2)}) copy-start(bf16[512,1024]{1,0:T(8,128)(2,1)} %constant.5.clone.band_ref) | copy-start | bytes 3145732

commit v6 on v5

--- a/solution.py
+++ b/solution.py
@@ -261,7 +261,7 @@
     ang_ref[...] = bins(NBLOCK).astype(jnp.float32) * jnp.float32(2.0 * math.pi / samples)
 
     me = lax.axis_index("pair")
-    slot = jnp.where(me == order[0], 0, jnp.where(me < order[0], me + 1, me))
+    slot = sum(jnp.where(me == pair, index, 0) for index, pair in enumerate(order))
     first_channel = (lax.axis_index("row") * shards + slot) * own
     diagonal = lax.broadcasted_iota(jnp.int32, (NBLOCK, NBLOCK), 0) == lax.broadcasted_iota(
         jnp.int32, (NBLOCK, NBLOCK), 1
@@ -467,8 +467,7 @@
     own = channels // shards
     height = own * NBLOCK + own * NBLOCK // 2
     basis, band = band_factors(length, samples)
-    lead = shards // 2
-    order = (lead, *range(lead), *range(lead + 1, shards))
+    order = tuple((shards // 2 + 1 + place) % shards for place in range(shards))
 
     by_owner = jnp.transpose(records, (0, 2, 1)).reshape(channels * NBLOCK, length)
     blank = pl.pallas_call(

time: 26.9 us -> 26.2 us (0.974)
  blocking collectives: 23.3 us -> 22.6 us
    all_to_all x1, blocking collectives: 12.2 us -> 11.5 us  [per_device(): lax.all_to_all(payload, 'pair', split_axis=0, concat_axis=0, tiled=True,...]
where the time goes in v6:
time: 26.2 us; the launch traced here: 26 us
  blocking collectives  22.6 us (86%)
  Pallas kernels  2.52 us (10%)
  between operations  0.83 us (3%)
    all_to_all x1, blocking collectives, per_device(): lax.all_to_all(payload, 'pair', split_axis=0, concat_axis=0, tiled=True,...  11.5 us
    all_to_all x1, blocking collectives, per_device(): lax.all_to_all(stats, ('pair', 'row'), split_axis=0, concat_axis=0, tiled...  11.1 us
    pallas_call x1, Pallas kernels, per_device(): pl.pallas_call(functools.partial(stats_kernel, order), out_shape=jax.Shap...  1.06 us
    pallas_call x1, Pallas kernels, per_device(): pl.pallas_call(functools.partial(solve_kernel, order, own, float(NBLOCK *...  0.81 us

profile of v6, /device:TPU:0, one launch (start us, length us, event | category | flops | bytes accessed | tf_op | source)
XLA Modules:
  0.0 26.0 jit_solution(9195236318696288125)
XLA Ops:
  0.0 0.0 copy-start.1
  0.0 0.0 copy-start.3
  0.0 0.0 copy-start.4
  0.0 0.0 copy-start.2
  0.0 0.0 copy-start
  0.8 0.0 copy-done.3
  0.8 0.0 copy-done.4
  0.8 0.4 %tables.1 = (f32[8,1024]{1,0:T(8,128)S(1)}, f32[8,512]{1,0:T(8,128)S(1)}, bf16[256,512]{1,0:T(8,128)(2,1)S(1)}, f32[4,8,128]{2,1,0:T(8,128)S(1)}, f32[8,128]{1,0:T(8,128)S(1)}, /*index=5*/f32[8,128]{1,0:T(8,128)S(1)}) custom-call(s32[1,8]{1,0:T(1,128)S(1)} %bitcast.9, f32[1,1]{1,0:T(1,128)} %bitcast.6.damp_ref, f32[1,32]{1,0:T(1,128)S(1)} %copy-done.4, ...), custom_call_target="tpu_custom_call" | custom-call | tf_op jit(solution)/shard_map/tables/pallas_call | solution.py:483
  1.2 0.0 copy-done.1
  1.2 0.0 copy-done.2
  1.2 0.3 %pack.1 = bf16[8,48,128]{2,1,0:T(8,128)(2,1)S(1)} custom-call(bf16[256,512]{1,0:T(8,128)(2,1)S(1)} %bitcast.7, bf16[1024,256]{1,0:T(8,128)(2,1)S(1)} %copy-done.1, f32[8,128]{1,0:T(8,128)S(1)} %get-tuple-element.11.value_ref), custom_call_target="tpu_custom_call" | custom-call | tf_op jit(solution)/shard_map/pack/pallas_call | solution.py:499
  1.5 11.5 %all_to_all.10.x_ref = bf16[8,48,128]{2,1,0:T(8,128)(2,1)S(1)} all-to-all(bf16[8,48,128]{2,1,0:T(8,128)(2,1)S(1)} %pack.1), channel_id=1, replica_groups={{20,24,28,0,4,8,12,16},{21,25,29,1,5,9,13,17},{22,26,30,2,6,10,14,18},{..., dimensions={0} | all-to-all | bytes 196608 | tf_op jit(solution)/shard_map/all_to_all | solution.py:507
  13.0 0.0 copy-done
  13.0 1.1 %stats.1 = f32[32,2,128]{2,1,0:T(2,128)S(1)} custom-call(bf16[8,48,128]{2,1,0:T(8,128)(2,1)S(1)} %all_to_all.10.x_ref, bf16[512,1024]{1,0:T(8,128)(2,1)S(1)} %copy-done, f32[8,1024]{1,0:T(8,128)S(1)} %get-tuple-element.12.turn_ref, f32[8,512]{1,0:T(8,128)S(1)} %get-tuple-element.13.ang_ref, bf16[256,512]{1,0:T(8,128)(2,1)S(1)} %get-tuple-element.14.lag_ref, ...), custom_call_target="tpu_custom_call" | custom-call | tf_op jit(solution)/shard_map/stats/pallas_call | solution.py:511
  14.1 11.1 %all_to_all.11 = f32[32,2,128]{2,1,0:T(2,128)S(1)} all-to-all(f32[32,2,128]{2,1,0:T(2,128)S(1)} %stats.1), channel_id=1, replica_groups=mesh['pair'=8,'row'=4] {'pair','row'}, dimensions={0} | all-to-all | bytes 65536 | tf_op jit(solution)/shard_map/all_to_all | solution.py:520
  25.2 0.8 %solve.1 = f32[1,32]{1,0:T(1,128)} custom-call(f32[8,4,2,128]{3,2,1,0:T(2,128)S(1)} %bitcast.8, f32[8,128]{1,0:T(8,128)S(1)} %get-tuple-element.16.damp_ref), custom_call_target="tpu_custom_call" | custom-call | tf_op jit(solution)/shard_map/solve/pallas_call | solution.py:522
  (1 shorter events, 0.0 us)
Async XLA Ops:
  0.0 1.2 %copy-start.1 = (bf16[1024,256]{1,0:T(8,128)(2,1)S(1)}, bf16[1024,256]{1,0:T(8,128)(2,1)}, u32[]{:S(2)}) copy-start(bf16[1024,256]{1,0:T(8,128)(2,1)} %constant.4.clone.basis_ref) | copy-start | bytes 1572868
  0.0 0.8 %copy-start.3 = (s32[8]{0:T(128)S(1)}, s32[8]{0:T(128)}, u32[]{:S(2)}) copy-start(s32[8]{0:T(128)} %param.8) | copy-start | bytes 100
  0.0 0.8 %copy-start.4 = (f32[1,32]{1,0:T(1,128)S(1)}, f32[1,32]{1,0:T(1,128)}, u32[]{:S(2)}) copy-start(f32[1,32]{1,0:T(1,128)} %off_ref.1) | copy-start | bytes 388
  0.0 1.2 %copy-start.2 = (bf16[32,512,8]{1,2,0:T(8,128)(2,1)S(1)}, bf16[32,512,8]{1,2,0:T(8,128)(2,1)}, u32[]{:S(2)}) copy-start(bf16[32,512,8]{1,2,0:T(8,128)(2,1)} %param.6) | copy-start | bytes 786436
  0.0 13.0 %copy-start = (bf16[512,1024]{1,0:T(8,128)(2,1)S(1)}, bf16[512,1024]{1,0:T(8,128)(2,1)}, u32[]{:S(2)}) copy-start(bf16[512,1024]{1,0:T(8,128)(2,1)} %constant.5.clone.band_ref) | copy-start | bytes 3145732

commit v7 on v6

--- a/solution.py
+++ b/solution.py
@@ -139,7 +139,8 @@
 @functools.cache
 def band_factors(length, samples):
     times = np.arange(length, dtype=np.float64)
-    bins = samples // 8 + np.arange(NF)
+    place = np.arange(NF)
+    bins = samples // 8 + place % LANES * (NF // LANES) + place // LANES
     centre = samples // 8 + NF // 2
     main = ((length - 1 - 2 * times) / 2) ** 2 * math.cos(math.pi * NF / samples)
     side = times[1:] * (length - times[1:]) / 2
@@ -166,10 +167,6 @@
     return lax.broadcasted_iota(jnp.int32, (height, LANES), 1)
 
 
-def blank_kernel(out_ref):
-    out_ref[...] = jnp.zeros_like(out_ref)
-
-
 def pack_kernel(rec_ref, basis_ref, value_ref, out_ref):
     ndest = out_ref.shape[0]
     rows = rec_ref.shape[0] // ndest
@@ -219,47 +216,39 @@
     return 1.0 - 2.0 * sine * sine, 2.0 * sine * cosine
 
 
-def table_kernel(
-    order, samples, counts_ref, damp_ref, off_ref, blank_ref,
-    turn_ref, ang_ref, lag_ref, live_ref, wide_ref, value_ref, coarse,
+def band_ids(height):
+    place = lax.broadcasted_iota(jnp.int32, (height, NF), 1)
+    return lax.rem(place, LANES) * (NF // LANES) + lax.div(place, LANES)
+
+
+WAVE_ROWS = 16
+
+
+def wave_kernel(samples, fine_ref, coarse_ref, ang_ref, blank_ref):
+    first_bin = samples // 8
+
+    def bins(height):
+        return first_bin + band_ids(height)
+
+    ids = lax.broadcasted_iota(jnp.int32, (WAVE_ROWS, NF), 0)
+    centre = (band_ids(1).astype(jnp.float32) + 0.5) * (math.pi / NF)
+    _, weight = sin_cos(centre - jnp.float32(math.pi / 2))
+    factor = -2.0 * (weight * weight)
+    fine_cos, fine_sin = unit_circle(ids * bins(WAVE_ROWS), samples)
+    fine_ref[:, :NF] = fine_cos * factor
+    fine_ref[:, NF:] = fine_sin * factor
+    coarse_cos, coarse_sin = unit_circle((ids * WAVE_ROWS + 1) * bins(WAVE_ROWS), samples)
+    coarse_ref[:, :NF] = coarse_cos
+    coarse_ref[:, NF:] = coarse_sin
+    ang_ref[...] = bins(NBLOCK).astype(jnp.float32) * jnp.float32(2.0 * math.pi / samples)
+    blank_ref[...] = jnp.zeros_like(blank_ref)
+
+
+def small_kernel(
+    order, counts_ref, damp_ref, off_ref, blank_ref, live_ref, wide_ref, value_ref
 ):
     shards = len(order)
-    length = samples // shards
     own = live_ref.shape[0]
-    rows = 16
-    first_bin = samples // 8
-
-    def bins(height):
-        return first_bin + lax.broadcasted_iota(jnp.int32, (height, NF), 1)
-
-    def ids(height):
-        return lax.broadcasted_iota(jnp.int32, (height, NF), 0)
-
-    fine_cos, fine_sin = unit_circle(ids(rows) * bins(rows), samples)
-    lags = NLAG // rows
-    wide_cos, wide_sin = unit_circle((ids(lags) * rows + 1) * bins(lags), samples)
-    coarse[:, :NF] = wide_cos
-    coarse[:, NF:] = wide_sin
-    centre = (lax.broadcasted_iota(jnp.int32, (1, NF), 1).astype(jnp.float32) + 0.5) * (
-        math.pi / NF
-    )
-    _, weight = sin_cos(centre - jnp.float32(math.pi / 2))
-    factor = -2.0 * (weight * weight)
-    lag_cos = fine_cos * factor
-    lag_sin = fine_sin * factor
-
-    @pl.loop(0, lags)
-    def _(step):
-        row_cos = coarse[pl.ds(step, 1), :NF]
-        row_sin = coarse[pl.ds(step, 1), NF:]
-        at = pl.ds(pl.multiple_of(step * rows, rows), rows)
-        lag_ref[at, :] = (row_sin * lag_cos + row_cos * lag_sin).astype(jnp.bfloat16)
-
-    turn_cos, turn_sin = unit_circle(ids(shards) * length * bins(shards), samples)
-    turn_ref[:, :NF] = turn_cos
-    turn_ref[:, NF:] = turn_sin
-    ang_ref[...] = bins(NBLOCK).astype(jnp.float32) * jnp.float32(2.0 * math.pi / samples)
-
     me = lax.axis_index("pair")
     slot = sum(jnp.where(me == pair, index, 0) for index, pair in enumerate(order))
     first_channel = (lax.axis_index("row") * shards + slot) * own
@@ -277,8 +266,19 @@
     value_ref[:, :channels] = jnp.broadcast_to(off_ref[...], (NBLOCK, channels))
 
 
+def plus_turned(first, second, quarters):
+    (real, imag), (far_real, far_imag) = first, second
+    if quarters % 4 == 0:
+        return real + far_real, imag + far_imag
+    if quarters % 4 == 1:
+        return real - far_imag, imag + far_real
+    if quarters % 4 == 2:
+        return real - far_real, imag - far_imag
+    return real + far_imag, imag - far_real
+
+
 def stats_kernel(
-    order, x_ref, band_ref, turn_ref, ang_ref, lag_ref, live_ref, out_ref, stacked,
+    order, x_ref, band_ref, fine_ref, coarse_ref, ang_ref, live_ref, out_ref, stacked, lag_ref,
 ):
     shards = x_ref.shape[0]
     own = live_ref.shape[0]
@@ -303,13 +303,21 @@
     shift = (pieces + pltpu.roll(pieces, LANES - own, 1)) + pltpu.roll(
         pieces, LANES - 2 * own, 1
     )
+    for step in range(NLAG // WAVE_ROWS):
+        row_cos = coarse_ref[pl.ds(step, 1), :NF]
+        row_sin = coarse_ref[pl.ds(step, 1), NF:]
+        lag_ref[pl.ds(step * WAVE_ROWS, WAVE_ROWS), :] = (
+            row_sin * fine_ref[:, :NF] + row_cos * fine_ref[:, NF:]
+        ).astype(jnp.bfloat16)
+
     cols = NF // LANES
     spread = [shift[:, SPARE + c : SPARE + c + 1] for c in range(own)]
     rotations = [
         [sin_cos(spread[c] * ang_ref[:, col * LANES : (col + 1) * LANES]) for c in range(own)]
         for col in range(cols)
     ]
-    home = order.index(0)
+    sign = 1 - 2 * lax.bitwise_and(lanes_of(1), 1)
+    sign = sign.astype(jnp.float32)
     energy = [jnp.zeros((NBLOCK, LANES), jnp.float32)] * own
     reals = [[] for _ in range(own)]
     imags = [[] for _ in range(own)]
@@ -319,19 +327,22 @@
             band_ref[:, 2 * col * LANES : 2 * (col + 1) * LANES],
             preferred_element_type=jnp.float32,
         )
-        cut = slice(col * LANES, (col + 1) * LANES)
-        cut_sine = slice(NF + col * LANES, NF + (col + 1) * LANES)
-        cosine_part = spectrum[home * rows : (home + 1) * rows, :LANES]
-        sine_part = spectrum[home * rows : (home + 1) * rows, LANES:]
-        for shard in range(shards):
-            if shard == home:
-                continue
-            turn_cos = turn_ref[pl.ds(order[shard], 1), cut]
-            turn_sin = turn_ref[pl.ds(order[shard], 1), cut_sine]
-            part_cos = spectrum[shard * rows : (shard + 1) * rows, :LANES]
-            part_sin = spectrum[shard * rows : (shard + 1) * rows, LANES:]
-            cosine_part += turn_cos * part_cos - turn_sin * part_sin
-            sine_part += turn_sin * part_cos + turn_cos * part_sin
+
+        def shard(pair):
+            at = order.index(pair) * rows
+            return spectrum[at : at + rows, :LANES], spectrum[at : at + rows, LANES:]
+
+        def joined(pair):
+            return plus_turned(shard(pair), shard(pair + shards // 2), 2 * col)
+
+        low = plus_turned(joined(0), joined(2), col)
+        real, imag = plus_turned(joined(1), joined(3), col)
+        if col % 2:
+            root = sign * jnp.float32(math.sqrt(0.5))
+            odd = (real - imag) * root, (real + imag) * root
+        else:
+            odd = real * sign, imag * sign
+        cosine_part, sine_part = plus_turned(low, odd, col // 2)
         for c in range(own):
             piece = slice(c * NBLOCK, (c + 1) * NBLOCK)
             shift_sin, shift_cos = rotations[col][c]
@@ -362,13 +373,24 @@
             stacked[pl.ds(part * half + c * width, width), :] = jnp.concatenate(
                 [crossing[part] for crossing in crossings], axis=0
             ).astype(jnp.bfloat16)
-    lagged = lax.dot_general(
-        lag_ref[...], stacked[...], (((1,), (1,)), ((), ())), preferred_element_type=jnp.float32
-    )
-    residual = lagged[:, :half]
-    jacobian = lagged[:, half:]
-    squares = jnp.sum(jacobian * jacobian, axis=0, keepdims=True)
-    products = jnp.sum(jacobian * residual, axis=0, keepdims=True)
+    sums = []
+    for part in range(2):
+        lagged = lax.dot_general(
+            lag_ref[pl.ds(part * (NLAG // 2), NLAG // 2), :],
+            stacked[...],
+            (((1,), (1,)), ((), ())),
+            preferred_element_type=jnp.float32,
+        )
+        residual = lagged[:, :half]
+        jacobian = lagged[:, half:]
+        sums.append(
+            (
+                jnp.sum(jacobian * jacobian, axis=0, keepdims=True),
+                jnp.sum(jacobian * residual, axis=0, keepdims=True),
+            )
+        )
+    squares = sums[0][0] + sums[1][0]
+    products = sums[0][1] + sums[1][1]
     both = jnp.concatenate([squares, products], axis=0)
     out_ref[...] = jnp.broadcast_to(both[None], out_ref.shape)
 
@@ -470,31 +492,32 @@
     order = tuple((shards // 2 + 1 + place) % shards for place in range(shards))
 
     by_owner = jnp.transpose(records, (0, 2, 1)).reshape(channels * NBLOCK, length)
-    blank = pl.pallas_call(
-        blank_kernel,
-        out_shape=jax.ShapeDtypeStruct((NBLOCK, LANES), jnp.float32),
-        out_specs=VMEM,
+    *waves, blank = pl.pallas_call(
+        functools.partial(wave_kernel, samples),
+        out_shape=(
+            jax.ShapeDtypeStruct((WAVE_ROWS, 2 * NF), jnp.float32),
+            jax.ShapeDtypeStruct((WAVE_ROWS, 2 * NF), jnp.float32),
+            jax.ShapeDtypeStruct((NBLOCK, NF), jnp.float32),
+            jax.ShapeDtypeStruct((NBLOCK, LANES), jnp.float32),
+        ),
+        out_specs=(VMEM,) * 4,
         compiler_params=room(4),
         cost_estimate=pl.CostEstimate(
             flops=20000000000, bytes_accessed=40000000, transcendentals=0
         ),
-        name="blank",
+        name="waves",
     )()
-    *tables, wide, value = pl.pallas_call(
-        functools.partial(table_kernel, order, samples),
+    live, wide, value = pl.pallas_call(
+        functools.partial(small_kernel, order),
         out_shape=(
-            jax.ShapeDtypeStruct((shards, 2 * NF), jnp.float32),
-            jax.ShapeDtypeStruct((NBLOCK, NF), jnp.float32),
-            jax.ShapeDtypeStruct((NLAG, NF), jnp.bfloat16),
             jax.ShapeDtypeStruct((own, NBLOCK, LANES), jnp.float32),
             jax.ShapeDtypeStruct((NBLOCK, LANES), jnp.float32),
             jax.ShapeDtypeStruct((NBLOCK, LANES), jnp.float32),
         ),
         in_specs=[VMEM] * 4,
-        out_specs=(VMEM,) * 6,
-        scratch_shapes=[pltpu.VMEM((NLAG // 16, 2 * NF), jnp.float32)],
-        compiler_params=room(8),
-        name="tables",
+        out_specs=(VMEM,) * 3,
+        compiler_params=room(4),
+        name="small",
     )(counts[None, :], damping[None, :], offsets, blank)
     payload = pl.pallas_call(
         pack_kernel,
@@ -513,10 +536,13 @@
         out_shape=jax.ShapeDtypeStruct((shards * rows, 2, LANES), jnp.float32),
         in_specs=[VMEM] * 6,
         out_specs=VMEM,
-        scratch_shapes=[pltpu.VMEM((2 * own * REACH * NBLOCK, NF), jnp.bfloat16)],
+        scratch_shapes=[
+            pltpu.VMEM((2 * own * REACH * NBLOCK, NF), jnp.bfloat16),
+            pltpu.VMEM((NLAG, NF), jnp.bfloat16),
+        ],
         compiler_params=room(12),
         name="stats",
-    )(received, jnp.asarray(band), *tables)
+    )(received, jnp.asarray(band), *waves, live)
     gathered = lax.all_to_all(stats, ("pair", "row"), split_axis=0, concat_axis=0, tiled=True)
     gathered = gathered.reshape(shards, rows, 2, LANES)
     return pl.pallas_call(
@@ -535,7 +561,7 @@
     channels, length, nblock = records.shape
     own = channels // shards
     whole = own * shards == channels and own * REACH * NBLOCK == LANES
-    even = length & (length - 1) == 0 and length == NF
+    even = length & (length - 1) == 0 and length == NF == 4 * LANES
     if shards == NBLOCK and nblock == NBLOCK and whole and even:
         return per_device(records, offsets, counts, damping)
     return per_device_general(records, offsets, counts, damping)

time: 26.2 us -> 26.1 us (level)
  no operation moved by 1% of the time
where the time goes in v7:
time: 26.1 us; the launch traced here: 25.9 us
  blocking collectives  22.6 us (87%)
  Pallas kernels  2.28 us (9%)
  between operations  0.81 us (3%)
    all_to_all x1, blocking collectives, per_device(): lax.all_to_all(payload, 'pair', split_axis=0, concat_axis=0, tiled=True,...  11.5 us
    all_to_all x1, blocking collectives, per_device(): lax.all_to_all(stats, ('pair', 'row'), split_axis=0, concat_axis=0, tiled...  11.1 us
    pallas_call x1, Pallas kernels, per_device(): pl.pallas_call(functools.partial(stats_kernel, order), out_shape=jax.Shap...  0.98 us
    pallas_call x1, Pallas kernels, per_device(): pl.pallas_call(functools.partial(solve_kernel, order, own, float(NBLOCK *...  0.81 us

profile of v7, /device:TPU:0, one launch (start us, length us, event | category | flops | bytes accessed | tf_op | source)
XLA Modules:
  0.0 25.9 jit_solution(1658788279261170092)
XLA Ops:
  0.0 0.0 copy-start.1
  0.0 0.0 copy-start.3
  0.0 0.0 copy-start.4
  0.0 0.0 copy-start.2
  0.0 0.1 waves.1
  0.1 0.0 copy-start
  0.9 0.0 copy-done.3
  0.9 0.0 copy-done.4
  0.9 0.1 small.1
  1.0 0.1 copy-done.1
  1.1 0.1 copy-done.2
  1.2 0.3 %pack.1 = bf16[8,48,128]{2,1,0:T(8,128)(2,1)S(1)} custom-call(bf16[256,512]{1,0:T(8,128)(2,1)S(1)} %bitcast.7, bf16[1024,256]{1,0:T(8,128)(2,1)S(1)} %copy-done.1, f32[8,128]{1,0:T(8,128)S(1)} %get-tuple-element.13.value_ref), custom_call_target="tpu_custom_call" | custom-call | tf_op jit(solution)/shard_map/pack/pallas_call | solution.py:522
  1.5 11.5 %all_to_all.10.x_ref = bf16[8,48,128]{2,1,0:T(8,128)(2,1)S(1)} all-to-all(bf16[8,48,128]{2,1,0:T(8,128)(2,1)S(1)} %pack.1), channel_id=1, replica_groups={{20,24,28,0,4,8,12,16},{21,25,29,1,5,9,13,17},{22,26,30,2,6,10,14,18},{..., dimensions={0} | all-to-all | bytes 196608 | tf_op jit(solution)/shard_map/all_to_all | solution.py:530
  13.0 0.0 copy-done
  13.0 1.0 %stats.1 = f32[32,2,128]{2,1,0:T(2,128)S(1)} custom-call(bf16[8,48,128]{2,1,0:T(8,128)(2,1)S(1)} %all_to_all.10.x_ref, bf16[512,1024]{1,0:T(8,128)(2,1)S(1)} %copy-done, f32[16,1024]{1,0:T(8,128)S(1)} %get-tuple-element.14.fine_ref, f32[16,1024]{1,0:T(8,128)S(1)} %get-tuple-element.15.coarse_ref, f32[8,512]{1,0:T(8,128)S(1)} %get-tuple-element.16.ang_ref, ...), custom_call_target="tpu_custom_call" | custom-call | tf_op jit(solution)/shard_map/stats/pallas_call | solution.py:534
  14.0 11.1 %all_to_all.11 = f32[32,2,128]{2,1,0:T(2,128)S(1)} all-to-all(f32[32,2,128]{2,1,0:T(2,128)S(1)} %stats.1), channel_id=1, replica_groups=mesh['pair'=8,'row'=4] {'pair','row'}, dimensions={0} | all-to-all | bytes 65536 | tf_op jit(solution)/shard_map/all_to_all | solution.py:546
  25.1 0.8 %solve.1 = f32[1,32]{1,0:T(1,128)} custom-call(f32[8,4,2,128]{3,2,1,0:T(2,128)S(1)} %bitcast.8, f32[8,128]{1,0:T(8,128)S(1)} %get-tuple-element.18.damp_ref), custom_call_target="tpu_custom_call" | custom-call | tf_op jit(solution)/shard_map/solve/pallas_call | solution.py:548
Async XLA Ops:
  0.0 1.1 %copy-start.1 = (bf16[1024,256]{1,0:T(8,128)(2,1)S(1)}, bf16[1024,256]{1,0:T(8,128)(2,1)}, u32[]{:S(2)}) copy-start(bf16[1024,256]{1,0:T(8,128)(2,1)} %constant.4.clone.basis_ref) | copy-start | bytes 1572868
  0.0 0.9 %copy-start.3 = (s32[8]{0:T(128)S(1)}, s32[8]{0:T(128)}, u32[]{:S(2)}) copy-start(s32[8]{0:T(128)} %param.8) | copy-start | bytes 100
  0.0 0.9 %copy-start.4 = (f32[1,32]{1,0:T(1,128)S(1)}, f32[1,32]{1,0:T(1,128)}, u32[]{:S(2)}) copy-start(f32[1,32]{1,0:T(1,128)} %off_ref.1) | copy-start | bytes 388
  0.0 1.1 %copy-start.2 = (bf16[32,512,8]{1,2,0:T(8,128)(2,1)S(1)}, bf16[32,512,8]{1,2,0:T(8,128)(2,1)}, u32[]{:S(2)}) copy-start(bf16[32,512,8]{1,2,0:T(8,128)(2,1)} %param.6) | copy-start | bytes 786436
  0.1 12.9 %copy-start = (bf16[512,1024]{1,0:T(8,128)(2,1)S(1)}, bf16[512,1024]{1,0:T(8,128)(2,1)}, u32[]{:S(2)}) copy-start(bf16[512,1024]{1,0:T(8,128)(2,1)} %constant.5.clone.band_ref) | copy-start | bytes 3145732

commit v8 on v7

--- a/solution.py
+++ b/solution.py
@@ -180,10 +180,14 @@
     first = lanes_of(late) < HALF
     plain = (lanes_of(late) < SPARE) | (lanes_of(late) >= SPARE + 3 * own)
     signal = rec_ref[...]
-    found = jnp.dot(
-        jnp.concatenate([signal, signal], axis=1),
-        basis_ref[...],
-        preferred_element_type=jnp.float32,
+    twice = jnp.concatenate([signal, signal], axis=1)
+    middle = ndest // 2 * rows
+    found = jnp.concatenate(
+        [
+            jnp.dot(part, basis_ref[...], preferred_element_type=jnp.float32)
+            for part in (twice[:middle], twice[middle:])
+        ],
+        axis=0,
     )
     for dest in range(ndest):
         tile = jnp.zeros_like(value)

time: 26.1 us -> 26.1 us (level)
  no operation moved by 1% of the time
where the time goes in v8:
time: 26.1 us; the launch traced here: 25.9 us
  blocking collectives  22.6 us (87%)
  Pallas kernels  2.29 us (9%)
  between operations  0.81 us (3%)
    all_to_all x1, blocking collectives, per_device(): lax.all_to_all(payload, 'pair', split_axis=0, concat_axis=0, tiled=True,...  11.5 us
    all_to_all x1, blocking collectives, per_device(): lax.all_to_all(stats, ('pair', 'row'), split_axis=0, concat_axis=0, tiled...  11.1 us
    pallas_call x1, Pallas kernels, per_device(): pl.pallas_call(functools.partial(stats_kernel, order), out_shape=jax.Shap...  0.98 us
    pallas_call x1, Pallas kernels, per_device(): pl.pallas_call(functools.partial(solve_kernel, order, own, float(NBLOCK *...  0.81 us

profile of v8, /device:TPU:0, one launch (start us, length us, event | category | flops | bytes accessed | tf_op | source)
XLA Modules:
  0.0 25.9 jit_solution(6635494610835965594)
XLA Ops:
  0.0 0.0 copy-start.1
  0.0 0.0 copy-start.3
  0.0 0.0 copy-start.4
  0.0 0.0 copy-start.2
  0.0 0.1 waves.1
  0.1 0.0 copy-start
  0.9 0.0 copy-done.3
  0.9 0.0 copy-done.4
  0.9 0.1 small.1
  1.0 0.1 copy-done.1
  1.1 0.1 copy-done.2
  1.2 0.3 %pack.1 = bf16[8,48,128]{2,1,0:T(8,128)(2,1)S(1)} custom-call(bf16[256,512]{1,0:T(8,128)(2,1)S(1)} %bitcast.7, bf16[1024,256]{1,0:T(8,128)(2,1)S(1)} %copy-done.1, f32[8,128]{1,0:T(8,128)S(1)} %get-tuple-element.13.value_ref), custom_call_target="tpu_custom_call" | custom-call | tf_op jit(solution)/shard_map/pack/pallas_call | solution.py:526
  1.5 11.5 %all_to_all.10.x_ref = bf16[8,48,128]{2,1,0:T(8,128)(2,1)S(1)} all-to-all(bf16[8,48,128]{2,1,0:T(8,128)(2,1)S(1)} %pack.1), channel_id=1, replica_groups={{20,24,28,0,4,8,12,16},{21,25,29,1,5,9,13,17},{22,26,30,2,6,10,14,18},{..., dimensions={0} | all-to-all | bytes 196608 | tf_op jit(solution)/shard_map/all_to_all | solution.py:534
  13.0 0.0 copy-done
  13.0 1.0 %stats.1 = f32[32,2,128]{2,1,0:T(2,128)S(1)} custom-call(bf16[8,48,128]{2,1,0:T(8,128)(2,1)S(1)} %all_to_all.10.x_ref, bf16[512,1024]{1,0:T(8,128)(2,1)S(1)} %copy-done, f32[16,1024]{1,0:T(8,128)S(1)} %get-tuple-element.14.fine_ref, f32[16,1024]{1,0:T(8,128)S(1)} %get-tuple-element.15.coarse_ref, f32[8,512]{1,0:T(8,128)S(1)} %get-tuple-element.16.ang_ref, ...), custom_call_target="tpu_custom_call" | custom-call | tf_op jit(solution)/shard_map/stats/pallas_call | solution.py:538
  14.0 11.1 %all_to_all.11 = f32[32,2,128]{2,1,0:T(2,128)S(1)} all-to-all(f32[32,2,128]{2,1,0:T(2,128)S(1)} %stats.1), channel_id=1, replica_groups=mesh['pair'=8,'row'=4] {'pair','row'}, dimensions={0} | all-to-all | bytes 65536 | tf_op jit(solution)/shard_map/all_to_all | solution.py:550
  25.1 0.8 %solve.1 = f32[1,32]{1,0:T(1,128)} custom-call(f32[8,4,2,128]{3,2,1,0:T(2,128)S(1)} %bitcast.8, f32[8,128]{1,0:T(8,128)S(1)} %get-tuple-element.18.damp_ref), custom_call_target="tpu_custom_call" | custom-call | tf_op jit(solution)/shard_map/solve/pallas_call | solution.py:552
Async XLA Ops:
  0.0 1.1 %copy-start.1 = (bf16[1024,256]{1,0:T(8,128)(2,1)S(1)}, bf16[1024,256]{1,0:T(8,128)(2,1)}, u32[]{:S(2)}) copy-start(bf16[1024,256]{1,0:T(8,128)(2,1)} %constant.4.clone.basis_ref) | copy-start | bytes 1572868
  0.0 0.9 %copy-start.3 = (s32[8]{0:T(128)S(1)}, s32[8]{0:T(128)}, u32[]{:S(2)}) copy-start(s32[8]{0:T(128)} %param.8) | copy-start | bytes 100
  0.0 0.9 %copy-start.4 = (f32[1,32]{1,0:T(1,128)S(1)}, f32[1,32]{1,0:T(1,128)}, u32[]{:S(2)}) copy-start(f32[1,32]{1,0:T(1,128)} %off_ref.1) | copy-start | bytes 388
  0.0 1.1 %copy-start.2 = (bf16[32,512,8]{1,2,0:T(8,128)(2,1)S(1)}, bf16[32,512,8]{1,2,0:T(8,128)(2,1)}, u32[]{:S(2)}) copy-start(bf16[32,512,8]{1,2,0:T(8,128)(2,1)} %param.6) | copy-start | bytes 786436
  0.1 12.9 %copy-start = (bf16[512,1024]{1,0:T(8,128)(2,1)S(1)}, bf16[512,1024]{1,0:T(8,128)(2,1)}, u32[]{:S(2)}) copy-start(bf16[512,1024]{1,0:T(8,128)(2,1)} %constant.5.clone.band_ref) | copy-start | bytes 3145732
